TPU v7x, 256 devices: a whole 4x4x8 slice. The times are simulated.
256 devices in a mesh: dp: 16 (over x, y_hi, core), tensor: 16 (over y_lo, z).
Axes of the slice: x: 4, y: 4 (y_hi: 2, y_lo: 2; y = y_hi * 2 + y_lo), z: 8, core: 2. Of those that a mesh axis runs over, the one named last changes fastest.
Arguments:
- inputs: bfloat16 [8192, 6144], P(('dp', 'tensor')), may hold values from -36 to 36
- gain: float32 [6144], replicated, may hold values from 0.25 to 1.75
- w_in: bfloat16 [6144, 12288], P(None, 'tensor'), may hold values from -0.078125 to 0.078125
- grad_act: bfloat16 [8192, 12288], P('dp', 'tensor'), may hold values from -6 to 6
- residual_gradient: bfloat16 [8192, 6144], P(('dp', 'tensor')), may hold values from -6 to 6
Outputs:
- block_input_gradient: bfloat16 [8192, 6144], P(('dp', 'tensor'))
- grad_w: float32 [6144, 12288], P('dp', 'tensor')
- scale_gradient: float32 [6144], replicated
All inputs are finite; a program needn't handle non-finite values.
Results may differ from a plain program's by a relative error of at most 0.022.
Values may be sent and summed in bfloat16 or wider, within the bound.
No kernel may reach another device: no remote copies, remote signals or barrier semaphores. Data moves between devices by JAX's collectives and lax.ppermute only.
A program may use at most 128 MiB of HBM per device.

v0:
```python
import jax
import jax.numpy as jnp
from jax import lax
from jax.experimental import pallas as pl
from jax.experimental.pallas import tpu as pltpu
from jax.sharding import PartitionSpec as P

F32 = jnp.float32
BF16 = jnp.bfloat16
ROWS = 32
NZ = 8
CH = 384


def ppermute(value, axis, target):
    return lax.ppermute(value, axis, [(i, target(i)) for i in range(16)])


def z_shift(step):
    return lambda i: (i // NZ) * NZ + (i + step) % NZ


def to_z(value, step):
    return ppermute(value, "tensor", z_shift(step))


def swap_y(value):
    return ppermute(value, "tensor", lambda i: i ^ 8)


def to_x(value, step):
    return ppermute(value, "dp", lambda i: (i + 4 * step) % 16)


def swap_yh(value):
    return ppermute(value, "dp", lambda i: i ^ 2)


def swap_core(value):
    return ppermute(value, "dp", lambda i: i ^ 1)


def add(*terms):
    total = terms[0].astype(F32)
    for term in terms[1:]:
        total = total + term.astype(F32)
    return total.astype(BF16)


GROUPS = (
    (("A", 0), ("A", 1), ("A", -1), ("B", 0)),
    (("A", 2), ("A", -2), ("B", 1)),
    (("A", 3), ("A", -3), ("B", 2)),
    (("B", 3), ("A", 4), ("B", -2)),
    (("B", 4), ("B", -3), ("B", -1)),
)


def from_up(value):
    return to_z(value, -1)


def from_down(value):
    return to_z(value, 1)


MOVES = (
    ((("A", 1), from_up, ("A", 0)), (("A", -1), from_down, ("A", 0)), (("B", 0), swap_y, ("A", 0))),
    ((("A", 2), from_up, ("A", 1)), (("A", -2), from_down, ("A", -1)), (("B", 1), swap_y, ("A", 1))),
    ((("B", 2), swap_y, ("A", 2)), (("A", 3), from_up, ("A", 2)), (("A", -3), from_down, ("A", -2))),
    ((("B", 3), from_up, ("B", 2)), (("A", 4), from_down, ("A", -3)), (("B", -2), swap_y, ("A", -2))),
    ((("B", 4), from_up, ("B", 3)), (("B", -3), from_down, ("B", -2)), (("B", -1), swap_y, ("A", -1))),
)
def together(*values):
    return lax.optimization_barrier(values)


SMALL = pl.CostEstimate(flops=1, bytes_accessed=1, transcendentals=0)


def gelu_slope(value):
    scale = 0.7978845608028654
    square = value * value
    tanh = jnp.tanh(scale * (value + 0.044715 * (square * value)))
    return 0.5 * (1.0 + tanh) + 0.5 * value * (1.0 - tanh * tanh) * scale * (1.0 + 0.134145 * square)


def forward_kernel(slots, *refs):
    n = (len(refs) - 3) // 2
    tokens, w_ref, acts = refs[:n], refs[n], refs[n + 1 : 2 * n + 1]
    out_ref, total = refs[-2:]
    step = pl.program_id(0)
    term = jnp.dot(
        jnp.concatenate([block[...] for block in tokens], 0), w_ref[...], preferred_element_type=F32
    )

    @pl.when(step == 0)
    def _():
        total[...] = term

    @pl.when(step > 0)
    def _():
        total[...] += term

    @pl.when(step == pl.num_programs(0) - 1)
    def _():
        for at, act in enumerate(acts):
            rows = pl.ds(at * ROWS, ROWS)
            out_ref[rows, :] = (act[...].astype(F32) * gelu_slope(total[rows, :])).astype(BF16)


def forward(slots, tokens, w_in, grad_act):
    n = len(tokens)
    depth, width = w_in.shape
    part = depth // 4

    def act_spec(at):
        return pl.BlockSpec((ROWS, width), lambda j, o: (o[at], 0))

    return pl.pallas_call(
        forward_kernel,
        grid_spec=pltpu.PrefetchScalarGridSpec(
            num_scalar_prefetch=1,
            grid=(4,),
            in_specs=[pl.BlockSpec((ROWS, part), lambda j, o: (0, j))] * n
            + [pl.BlockSpec((part, width), lambda j, o: (j, 0))]
            + [act_spec(at) for at in range(n)],
            out_specs=pl.BlockSpec((n * ROWS, width), lambda j, o: (0, 0)),
            scratch_shapes=[pltpu.VMEM((n * ROWS, width), F32)],
        ),
        out_shape=jax.ShapeDtypeStruct((n * ROWS, width), BF16),
        compiler_params=pltpu.CompilerParams(vmem_limit_bytes=12 * 2**20),
        cost_estimate=SMALL,
        name="forward",
    )(slots, *tokens, w_in, *([grad_act] * n))


def backward(dpre, w_in):
    return lax.dot_general(
        dpre, w_in, (((1,), (1,)), ((), ())), preferred_element_type=F32
    ).astype(BF16)


def weight_kernel(order, place, *refs):
    blocks, rights = refs[:16], refs[16:-4]
    mine, theirs, left, turned = refs[-4:]

    @pl.when(pl.program_id(0) == 0)
    def _():
        turned[...] = jnp.concatenate([right[...] for right in rights], 0).T

    for at, block in enumerate(blocks):
        left[pl.ds(at * ROWS, ROWS), :] = block[...]
    product = jnp.dot(turned[...], left[...], preferred_element_type=F32).astype(BF16)
    for c in range(2):
        piece = product[:, c * CH : (c + 1) * CH]

        @pl.when(place[1] == c)
        def _():
            mine[0] = piece

        @pl.when(place[1] != c)
        def _():
            theirs[0] = piece


def weight_terms(order, place, blocks, rights):
    width = rights[0].shape[1]
    count = 2 * order.shape[0]
    specs = [
        pl.BlockSpec((ROWS, 2 * CH), lambda j, o, p: (0, 2 * o[j // 2] + (p[0] ^ 1 ^ (j % 2))))
    ] * 16
    specs += [pl.BlockSpec((right.shape[0], width), lambda j, o, p: (0, 0)) for right in rights]
    shape = jax.ShapeDtypeStruct((count, width, CH), BF16)
    return pl.pallas_call(
        weight_kernel,
        grid_spec=pltpu.PrefetchScalarGridSpec(
            num_scalar_prefetch=2,
            grid=(count,),
            in_specs=specs,
            out_specs=[pl.BlockSpec((1, width, CH), lambda j, o, p: (j, 0, 0))] * 2,
            scratch_shapes=[pltpu.VMEM((16 * ROWS, 2 * CH), BF16), pltpu.VMEM((width, 16 * ROWS), BF16)],
        ),
        out_shape=[shape, shape],
        compiler_params=pltpu.CompilerParams(vmem_limit_bytes=60 * 2**20),
        cost_estimate=pl.CostEstimate(
            flops=8 * 16 * ROWS * 2 * CH * count * width,
            bytes_accessed=2 * count * 2 * CH * (16 * ROWS + width),
            transcendentals=0,
        ),
        name="weight_terms",
    )(order, place, *blocks, *rights)


def place_kernel(slots, *refs):
    sources, board, sems = refs[:-2], refs[-2], refs[-1]
    copies = []
    for source in sources:
        for row in range(0, source.shape[0], ROWS):
            at = len(copies)
            into = pl.multiple_of(slots[at] * ROWS, ROWS)
            copies.append(
                pltpu.make_async_copy(
                    source.at[pl.ds(row, ROWS)], board.at[pl.ds(into, ROWS)], sems.at[at]
                )
            )
            copies[-1].start()
    for copy in copies:
        copy.wait()


def place_rows(slots, sources):
    return pl.pallas_call(
        place_kernel,
        in_specs=[pl.BlockSpec(memory_space=pltpu.SMEM)]
        + [pl.BlockSpec(memory_space=pl.ANY)] * len(sources),
        out_specs=pl.BlockSpec(memory_space=pl.ANY),
        out_shape=jax.ShapeDtypeStruct((16 * ROWS, sources[0].shape[1]), BF16),
        scratch_shapes=[pltpu.SemaphoreType.DMA((16,))],
        compiler_params=pltpu.CompilerParams(vmem_limit_bytes=2**20),
        cost_estimate=SMALL,
        name="place_rows",
    )(slots, *sources)


def scale_kernel(slots, *refs):
    blocks, product, out_ref = refs[:16], refs[16], refs[17]
    total = jnp.zeros(out_ref.shape, F32)
    for at, block in enumerate(blocks):
        row = pl.multiple_of(slots[at] * ROWS, ROWS)
        for tile in range(0, ROWS, 16):
            left = block[pl.ds(tile, 16), :].astype(F32)
            right = product[pl.ds(row + tile, 16), :].astype(F32)
            term = left * right
            total = total + term[:8] + term[8:]
    out_ref[...] = total


def scale_sum(slots, blocks, product):
    width = product.shape[1]
    cols = 1024
    return pl.pallas_call(
        scale_kernel,
        grid_spec=pltpu.PrefetchScalarGridSpec(
            num_scalar_prefetch=1,
            grid=(width // cols,),
            in_specs=[pl.BlockSpec((v.shape[0], cols), lambda j, o: (0, j)) for v in (*blocks, product)],
            out_specs=pl.BlockSpec((8, cols), lambda j, o: (0, j)),
        ),
        out_shape=jax.ShapeDtypeStruct((8, width), F32),
        compiler_params=pltpu.CompilerParams(vmem_limit_bytes=60 * 2**20),
        cost_estimate=SMALL,
        name="scale_sum",
    )(slots, *blocks, product)


def on_device(inputs, gain, w_in, grad_act, residual_gradient):
    dp_index = lax.axis_index("dp")
    t_index = lax.axis_index("tensor")
    x_at, yh_at, c_at = dp_index // 4, (dp_index // 2) % 2, dp_index % 2
    y_at, z_at = t_index // NZ, t_index % NZ

    with jax.named_scope("norm"):
        values = inputs.astype(F32)
        centered_input = values - jnp.mean(values, axis=1, keepdims=True)
        inverse_deviation = lax.rsqrt(
            jnp.mean(centered_input * centered_input, axis=1, keepdims=True) + 1e-06
        )
        standardized_input = centered_input * inverse_deviation
        normed_output = (standardized_input * gain).astype(BF16)

    def slots(keys):
        places = [
            (y_at if column == "A" else 1 - y_at) * NZ + (z_at + offset) % NZ for column, offset in keys
        ]
        return jnp.stack(places).astype(jnp.int32)

    got = {("A", 0): normed_output}
    rights = []

    def dense(at):
        rights.append(forward(slots(GROUPS[at]), [got[key] for key in GROUPS[at]], w_in, grad_act))

    with jax.named_scope("gather"):
        for at, moves in enumerate(MOVES):
            for key, move, source in moves:
                got[key] = move(got[source])
            along_z = [key for key, move, _ in moves if move is not swap_y]
            held = [got[key] for key in along_z]
            if at >= 1:
                dense(at - 1)
                held.append(rights[-1])
            later = [source for _, move, source in MOVES[at + 1] if move is swap_y] if at < 4 else []
            held = list(together(*held, *[got[key] for key in later if key not in along_z]))
            for key in along_z:
                got[key] = held.pop(0)
            for key in later:
                if key not in along_z:
                    got[key] = held.pop()
            if at >= 1:
                rights[-1] = held.pop(0)

    with jax.named_scope("turn"):
        dense(4)
        blocks = [got[key] for keys in GROUPS for key in keys]
        rows = slots([key for keys in GROUPS for key in keys])
        product = backward(place_rows(rows, rights), w_in)

    with jax.named_scope("scatter"):
        normed_gradient = lax.psum_scatter(product, "tensor", scatter_dimension=0, tiled=True).astype(F32)

    place = jnp.stack([yh_at, c_at]).astype(jnp.int32)
    order = jnp.stack([(x_at + k) % 4 for k in (2, 1, 3, 0)]).astype(jnp.int32)
    half = w_in.shape[1] // 2

    def hop(total, axis, bit):
        return total + ppermute(total, axis, lambda i: i ^ bit)

    def moving(mine, theirs, far, chunk, way):
        first = add(mine[chunk, :half], theirs[chunk, :half], *([far[0]] if way > 0 else []))
        second = add(mine[chunk, half:], theirs[chunk, half:], *([far[0]] if way < 0 else []))
        return jnp.concatenate([first, second], 0)

    with jax.named_scope("weights"):
        first, second = together(order[:1], order[1:], product[:1, :1])[:2]
        far_mine, far_theirs = weight_terms(first, place, blocks, rights)
        sums = scale_sum(rows, blocks, product)
        total = jnp.sum(sums, axis=0).reshape(48, 128)
        far_mine, far_theirs, second, total = together(far_mine, far_theirs, second, total)
        mine, theirs = weight_terms(second, place, blocks, rights)
        total = hop(hop(total, "dp", 1), "tensor", 1)
        far_mine, far_theirs, mine, theirs, total = together(far_mine, far_theirs, mine, theirs, total)

    with jax.named_scope("core_far"):
        (swapped,) = together(swap_core(far_theirs))
        far, theirs, total = together(add(far_mine, swapped), theirs, total)

    with jax.named_scope("x_far"):
        far_up, far_down = to_x(far[:, :half], 1), to_x(far[:, half:], -1)
        theirs = swap_core(theirs)
        total = hop(hop(hop(total, "tensor", 2), "tensor", 4), "dp", 4)
        far_up, far_down, theirs, total = together(far_up, far_down, theirs, total)

    with jax.named_scope("x_other"):
        up_other, down_other = moving(mine, theirs, far_up[:1], 0, 1), moving(mine, theirs, far_down[:1], 2, -1)
        up_other, down_other, total = together(up_other, down_other, total)
        up_moved, down_moved = to_x(up_other, 1), to_x(down_other, -1)
        up_own, down_own = moving(mine, theirs, far_up[1:], 1, 1), moving(mine, theirs, far_down[1:], 3, -1)
        total = hop(hop(total, "dp", 8), "dp", 2)
        up_moved, down_moved, up_own, down_own, total = together(
            up_moved, down_moved, up_own, down_own, total
        )

    with jax.named_scope("x_own"):
        other = add(mine[4], theirs[4], up_moved, down_moved)
        up_own, down_own, other, total = together(up_own, down_own, other, total)
        from_y = swap_yh(other)
        up_moved, down_moved = to_x(up_own, 1), to_x(down_own, -1)
        own = mine[5].astype(F32) + theirs[5].astype(F32)
        for value in (up_moved, down_moved, from_y):
            own = own + value.astype(F32)
        grad_w = (own / 16).T
        total = hop(total, "tensor", 8)
        scale_gradient = total.reshape(-1) / gain / 16

    with jax.named_scope("input_gradient"):
        scaled_gradient = normed_gradient * gain
        first_average = jnp.mean(scaled_gradient, axis=1, keepdims=True)
        second_average = jnp.mean(scaled_gradient * standardized_input, axis=1, keepdims=True)
        block_input_gradient = (
            residual_gradient.astype(F32)
            + inverse_deviation
            * (scaled_gradient - first_average - standardized_input * second_average)
        ).astype(BF16)
    return (block_input_gradient, grad_w, scale_gradient)


def solution(mesh):
    return jax.shard_map(
        on_device,
        mesh=mesh,
        in_specs=(
            P(("dp", "tensor"), None),
            P(),
            P(None, "tensor"),
            P("dp", "tensor"),
            P(("dp", "tensor"), None),
        ),
        out_specs=(P(("dp", "tensor"), None), P("dp", "tensor"), P()),
        check_vma=False,
    )
```

profile of v0, /device:TPU:4, one launch (start us, length us, event | category | flops | bytes accessed | tf_op | source)
XLA Modules:
  0.0 196.9 jit_solution(9586840518598807219)
XLA Ops:
  7.2 1.2 convert_reduce_fusion
  8.4 1.3 fusion.17
  9.7 1.2 fusion.11.refs_0_
  10.9 2.0 %collective-permute-start.1 = (bf16[32,6144]{1,0:T(8,128)(2,1)S(1)}, bf16[32,6144]{1,0:T(8,128)(2,1)}, u32[]{:S(2)}, u32[]{:S(2)}) collective-permute-start(bf16[32,6144]{1,0:T(8,128)(2,1)S(1)} %fusion.11.refs_0_), channel_id=1, source_target_pairs={{0,1},{1,2},{2,3},{3,4},{4,5},{5,6},{6,7},{7,0},{8,9},{9,10},{10,1... | collective-permute-start | bytes 1179656 | tf_op jit(solution)/shard_map/gather/ppermute | solution.py:16
  12.9 4.0 %collective-permute-start = (bf16[32,6144]{1,0:T(8,128)(2,1)S(1)}, bf16[32,6144]{1,0:T(8,128)(2,1)S(1)}, u32[]{:S(2)}, u32[]{:S(2)}) collective-permute-start(bf16[32,6144]{1,0:T(8,128)(2,1)S(1)} %fusion.11.refs_0_), channel_id=1, source_target_pairs={{0,7},{1,0},{2,1},{3,2},{4,3},{5,4},{6,5},{7,6},{8,15},{9,8},{10,9... | collective-permute-start | bytes 1179656 | tf_op jit(solution)/shard_map/gather/ppermute | solution.py:16
  17.0 1.6 collective-permute-start.4
  18.5 7.6 %collective-permute-done.1.refs_2_ = bf16[32,6144]{1,0:T(8,128)(2,1)} collective-permute-done((bf16[32,6144]{1,0:T(8,128)(2,1)S(1)}, bf16[32,6144]{1,0:T(8,128)(2,1)}, u32[]{:S(2)}, u32[]{:S(2)}) %collective-permute-start.1) | collective-permute-done | bytes 393248 | tf_op jit(solution)/shard_map/gather/ppermute | solution.py:16
  26.1 3.2 %collective-permute-start.2 = (bf16[32,6144]{1,0:T(8,128)(2,1)S(1)}, bf16[32,6144]{1,0:T(8,128)(2,1)S(1)}, u32[]{:S(2)}, u32[]{:S(2)}) collective-permute-start(bf16[32,6144]{1,0:T(8,128)(2,1)S(1)} %collective-permute-done.refs_1_), channel_id=1, source_target_pairs={{0,7},{1,0},{2,1},{3,2},{4,3},{5,4},{6,5},{7,6},{8,15},{9,8},{10,9... | collective-permute-start | bytes 1179656 | tf_op jit(solution)/shard_map/gather/ppermute | solution.py:16
  29.4 1.6 collective-permute-start.7
  31.0 3.7 %copy-done = bf16[6144,768]{1,0:T(8,128)(2,1)S(1)} copy-done((bf16[6144,768]{1,0:T(8,128)(2,1)S(1)}, bf16[6144,768]{1,0:T(8,128)(2,1)}, u32[]{:S(2)}) %copy-start) | copy-done | bytes 9437208
  34.7 4.3 %forward.5.refs_0_.refs_16_ = bf16[128,768]{1,0:T(8,128)(2,1)S(1)} custom-call(s32[4]{0:T(128)S(1)} %pad_add_fusion.slots, bf16[32,6144]{1,0:T(8,128)(2,1)S(1)} %fusion.11.refs_0_, bf16[32,6144]{1,0:T(8,128)(2,1)S(1)} %collective-permute-done.refs_1_, bf16[32,6144]{1,0:T(8,128)(2,1)} %collective-permute-done.1.refs_2_, ...), custom_call_target="tpu_custom_call" | custom-call | flops 1 | bytes 1 | tf_op jit(solution)/shard_map/gather/forward/pallas_call | solution.py:120
  39.0 0.7 copy-done.20
  39.8 3.2 %collective-permute-start.5 = (bf16[32,6144]{1,0:T(8,128)(2,1)S(1)}, bf16[32,6144]{1,0:T(8,128)(2,1)S(1)}, u32[]{:S(2)}, u32[]{:S(2)}) collective-permute-start(bf16[32,6144]{1,0:T(8,128)(2,1)S(1)} %collective-permute-done.2.refs_0_.refs_4_), channel_id=1, source_target_pairs={{0,7},{1,0},{2,1},{3,2},{4,3},{5,4},{6,5},{7,6},{8,15},{9,8},{10,9... | collective-permute-start | bytes 1179656 | tf_op jit(solution)/shard_map/gather/ppermute | solution.py:16
  43.0 0.4 collective-permute-start.8
  43.5 3.7 %copy-done.1 = bf16[6144,768]{1,0:T(8,128)(2,1)S(1)} copy-done((bf16[6144,768]{1,0:T(8,128)(2,1)S(1)}, bf16[6144,768]{1,0:T(8,128)(2,1)}, u32[]{:S(2)}) %copy-start.1) | copy-done | bytes 9437208
  47.2 3.1 %forward.6.refs_1_.refs_17_ = bf16[96,768]{1,0:T(8,128)(2,1)S(1)} custom-call(s32[3]{0:T(128)S(1)} %pad_add_fusion.1.slots, bf16[32,6144]{1,0:T(8,128)(2,1)S(1)} %collective-permute-done.2.refs_0_.refs_4_, bf16[32,6144]{1,0:T(8,128)(2,1)S(1)} %collective-permute-done.3.refs_1_.refs_5_, bf16[32,6144]{1,0:T(8,128)(2,1)S(1)} %collective-permute-done.7.refs_2_.refs_6_, ...), custom_call_target="tpu_custom_call" | custom-call | flops 1 | bytes 1 | tf_op jit(solution)/shard_map/gather/forward/pallas_call | solution.py:120
  50.3 0.7 copy-done.22
  51.0 0.9 collective-permute-done.8.refs_2_.refs_9_
  51.9 1.6 collective-permute-start.9
  53.5 0.5 collective-permute-start.10
  53.9 0.8 collective-permute-start.12
  54.8 3.7 %copy-done.2 = bf16[6144,768]{1,0:T(8,128)(2,1)S(1)} copy-done((bf16[6144,768]{1,0:T(8,128)(2,1)S(1)}, bf16[6144,768]{1,0:T(8,128)(2,1)}, u32[]{:S(2)}) %copy-start.2) | copy-done | bytes 9437208
  58.5 3.1 %forward.7.refs_2_.refs_18_ = bf16[96,768]{1,0:T(8,128)(2,1)S(1)} custom-call(s32[3]{0:T(128)S(1)} %pad_add_fusion.2.slots, bf16[32,6144]{1,0:T(8,128)(2,1)S(1)} %collective-permute-done.5.refs_0_.refs_7_, bf16[32,6144]{1,0:T(8,128)(2,1)S(1)} %collective-permute-done.6.refs_1_.refs_8_, bf16[32,6144]{1,0:T(8,128)(2,1)S(1)} %collective-permute-done.8.refs_2_.refs_9_, ...), custom_call_target="tpu_custom_call" | custom-call | flops 1 | bytes 1 | tf_op jit(solution)/shard_map/gather/forward/pallas_call | solution.py:120
  61.6 0.7 copy-done.24
  62.3 0.4 collective-permute-done.10.refs_1_.refs_11_
  62.8 3.2 %collective-permute-start.11 = (bf16[32,6144]{1,0:T(8,128)(2,1)S(1)}, bf16[32,6144]{1,0:T(8,128)(2,1)S(1)}, u32[]{:S(2)}, u32[]{:S(2)}) collective-permute-start(bf16[32,6144]{1,0:T(8,128)(2,1)S(1)} %collective-permute-done.9.refs_0_.refs_10_), channel_id=1, source_target_pairs={{0,7},{1,0},{2,1},{3,2},{4,3},{5,4},{6,5},{7,6},{8,15},{9,8},{10,9... | collective-permute-start | bytes 1179656 | tf_op jit(solution)/shard_map/gather/ppermute | solution.py:16
  66.0 0.9 collective-permute-start.14
  67.1 3.7 %copy-done.3 = bf16[6144,768]{1,0:T(8,128)(2,1)S(1)} copy-done((bf16[6144,768]{1,0:T(8,128)(2,1)S(1)}, bf16[6144,768]{1,0:T(8,128)(2,1)}, u32[]{:S(2)}) %copy-start.3) | copy-done | bytes 9437208
  70.8 3.1 %forward.8.refs_3_.refs_19_ = bf16[96,768]{1,0:T(8,128)(2,1)S(1)} custom-call(s32[3]{0:T(128)S(1)} %pad_add_fusion.3.slots, bf16[32,6144]{1,0:T(8,128)(2,1)S(1)} %collective-permute-done.9.refs_0_.refs_10_, bf16[32,6144]{1,0:T(8,128)(2,1)S(1)} %collective-permute-done.10.refs_1_.refs_11_, bf16[32,6144]{1,0:T(8,128)(2,1)S(1)} %collective-permute-done.12.refs_2_.refs_12_, ...), custom_call_target="tpu_custom_call" | custom-call | flops 1 | bytes 1 | tf_op jit(solution)/shard_map/gather/forward/pallas_call | solution.py:120
  74.0 3.1 %forward.9.refs_4_.refs_20_ = bf16[96,768]{1,0:T(8,128)(2,1)S(1)} custom-call(s32[3]{0:T(128)S(1)} %pad_add_fusion.4.slots, bf16[32,6144]{1,0:T(8,128)(2,1)S(1)} %collective-permute-done.11.refs_0_.refs_13_, bf16[32,6144]{1,0:T(8,128)(2,1)S(1)} %collective-permute-done.13.refs_1_.refs_14_, bf16[32,6144]{1,0:T(8,128)(2,1)S(1)} %collective-permute-done.14.refs_2_.refs_15_, ...), custom_call_target="tpu_custom_call" | custom-call | flops 1 | bytes 1 | tf_op jit(solution)/shard_map/turn/forward/pallas_call | solution.py:120
  77.2 1.8 place_rows.1
  79.1 7.0 %convolution_convert_fusion.refs_16_ = bf16[512,6144]{1,0:T(8,128)(2,1)} fusion(bf16[512,768]{1,0:T(8,128)(2,1)S(1)} %place_rows.1, bf16[6144,768]{1,0:T(8,128)(2,1)S(1)} %bitcast.64), kind=kOutput, calls=%fused_computation | convolution fusion | flops 4834983936 | bytes 16515072 | tf_op jit(solution)/shard_map/turn/dot_general | solution.py:139
  86.2 0.6 pad_add_fusion.5.order
  86.8 0.6 pad_add_fusion.6.place
  87.4 7.3 %scale_sum.1 = f32[8,6144]{1,0:T(8,128)} custom-call(s32[16]{0:T(128)} %copy-done.28, bf16[32,6144]{1,0:T(8,128)(2,1)} %copy-done.5, bf16[32,6144]{1,0:T(8,128)(2,1)} %copy-done.18, bf16[32,6144]{1,0:T(8,128)(2,1)} %collective-permute-done.1.refs_2_, bf16[32,6144]{1,0:T(8,128)(2,1)} %copy-done.19, bf16[32,6144]{1,0:T(8,128)(2,1)} %copy-done.7, ...), custom_call_target="tpu_custom_call" | custom-call | flops 1 | bytes 1 | tf_op jit(solution)/shard_map/weights/scale_sum/pallas_call | solution.py:242
  94.7 1.0 reduce_sum.49
  95.7 5.9 %weight_terms.2 = (bf16[2,768,384]{2,1,0:T(8,128)(2,1)}, bf16[2,768,384]{2,1,0:T(8,128)(2,1)}) custom-call(s32[1]{0:T(128)} %bitcast.16.order, s32[2]{0:T(128)} %pad_add_fusion.6.place, bf16[32,6144]{1,0:T(8,128)(2,1)} %copy-done.5, bf16[32,6144]{1,0:T(8,128)(2,1)} %copy-done.18, bf16[32,6144]{1,0:T(8,128)(2,1)} %collective-permute-done.1.refs_2_, ...), custom_call_target="tpu_custom_call" | custom-call | flops 4831838208 | bytes 3932160 | tf_op jit(solution)/shard_map/weights/weight_terms/pallas_call | solution.py:175
  101.7 1.2 collective-permute-done.15
  103.0 11.2 %weight_terms.3 = (bf16[6,768,384]{2,1,0:T(8,128)(2,1)}, bf16[6,768,384]{2,1,0:T(8,128)(2,1)}) custom-call(s32[3]{0:T(128)} %pad_add_fusion.5.order, s32[2]{0:T(128)} %pad_add_fusion.6.place, bf16[32,6144]{1,0:T(8,128)(2,1)} %copy-done.5, bf16[32,6144]{1,0:T(8,128)(2,1)} %copy-done.18, bf16[32,6144]{1,0:T(8,128)(2,1)} %collective-permute-done.1.refs_2_, ...), custom_call_target="tpu_custom_call" | custom-call | flops 14495514624 | bytes 11796480 | tf_op jit(solution)/shard_map/weights/weight_terms/pallas_call | solution.py:175
  114.5 2.7 %collective-permute-done.17 = bf16[2,768,384]{2,1,0:T(8,128)(2,1)S(1)} collective-permute-done((bf16[2,768,384]{2,1,0:T(8,128)(2,1)S(1)}, bf16[2,768,384]{2,1,0:T(8,128)(2,1)S(1)}, u32[]{:S(2)}, u32[]{:S(2)}) %collective-permute-start.17) | collective-permute-done | bytes 1179680 | tf_op jit(solution)/shard_map/core_far/ppermute | solution.py:16
  117.9 0.6 collective-permute-start.19
  118.6 1.5 collective-permute-start.18
  120.1 3.4 %collective-permute-start.21 = (f32[48,128]{1,0:T(8,128)S(1)}, f32[48,128]{1,0:T(8,128)S(1)}, u32[]{:S(2)}, u32[]{:S(2)}) collective-permute-start(f32[48,128]{1,0:T(8,128)S(1)} %add.351), channel_id=1, source_target_pairs={{0,2},{1,3},{2,0},{3,1},{4,6},{5,7},{6,4},{7,5},{8,10},{9,11},{10,... | collective-permute-start | bytes 73736 | tf_op jit(solution)/shard_map/x_far/ppermute | solution.py:16
  123.4 2.4 %collective-permute-done.21 = f32[48,128]{1,0:T(8,128)S(1)} collective-permute-done((f32[48,128]{1,0:T(8,128)S(1)}, f32[48,128]{1,0:T(8,128)S(1)}, u32[]{:S(2)}, u32[]{:S(2)}) %collective-permute-start.21) | collective-permute-done | bytes 24608 | tf_op jit(solution)/shard_map/x_far/ppermute | solution.py:16
  125.8 3.7 %collective-permute-start.22 = (f32[48,128]{1,0:T(8,128)S(1)}, f32[48,128]{1,0:T(8,128)S(1)}, u32[]{:S(2)}, u32[]{:S(2)}) collective-permute-start(f32[48,128]{1,0:T(8,128)S(1)} %add.353), channel_id=1, source_target_pairs={{0,4},{1,5},{2,6},{3,7},{4,0},{5,1},{6,2},{7,3},{8,12},{9,13},{10,... | collective-permute-start | bytes 73736 | tf_op jit(solution)/shard_map/x_far/ppermute | solution.py:16
  129.4 4.8 %collective-permute-done.22 = f32[48,128]{1,0:T(8,128)S(1)} collective-permute-done((f32[48,128]{1,0:T(8,128)S(1)}, f32[48,128]{1,0:T(8,128)S(1)}, u32[]{:S(2)}, u32[]{:S(2)}) %collective-permute-start.22) | collective-permute-done | bytes 24608 | tf_op jit(solution)/shard_map/x_far/ppermute | solution.py:16
  134.2 2.6 %collective-permute-start.23 = (f32[48,128]{1,0:T(8,128)S(1)}, f32[48,128]{1,0:T(8,128)S(1)}, u32[]{:S(2)}, u32[]{:S(2)}) collective-permute-start(f32[48,128]{1,0:T(8,128)S(1)} %add.354), channel_id=1, source_target_pairs={{0,64},{16,80},{32,96},{48,112},{64,0},{80,16},{96,32},{112,48},{1... | collective-permute-start | bytes 73736 | tf_op jit(solution)/shard_map/x_far/ppermute | solution.py:16
  136.9 1.8 collective-permute-done.23
  138.8 0.7 fusion.26
  139.7 2.1 %collective-permute-start.24 = (bf16[768,384]{1,0:T(8,128)(2,1)S(1)}, bf16[768,384]{1,0:T(8,128)(2,1)S(1)}, u32[]{:S(2)}, u32[]{:S(2)}) collective-permute-start(bf16[768,384]{1,0:T(8,128)(2,1)S(1)} %get-tuple-element.91), channel_id=1, source_target_pairs={{0,64},{16,80},{32,96},{48,112},{64,128},{80,144},{96,160},{112,17... | collective-permute-start | bytes 1769480 | tf_op jit(solution)/shard_map/x_other/ppermute | solution.py:16
  141.8 2.2 %collective-permute-start.26 = (f32[48,128]{1,0:T(8,128)S(1)}, f32[48,128]{1,0:T(8,128)S(1)}, u32[]{:S(2)}, u32[]{:S(2)}) collective-permute-start(f32[48,128]{1,0:T(8,128)S(1)} %add.355), channel_id=1, source_target_pairs={{0,128},{16,144},{32,160},{48,176},{64,192},{80,208},{96,224},{112... | collective-permute-start | bytes 73736 | tf_op jit(solution)/shard_map/x_other/ppermute | solution.py:16
  143.9 8.4 %collective-permute-done.26 = f32[48,128]{1,0:T(8,128)S(1)} collective-permute-done((f32[48,128]{1,0:T(8,128)S(1)}, f32[48,128]{1,0:T(8,128)S(1)}, u32[]{:S(2)}, u32[]{:S(2)}) %collective-permute-start.26) | collective-permute-done | bytes 24608 | tf_op jit(solution)/shard_map/x_other/ppermute | solution.py:16
  152.3 2.9 %collective-permute-start.27 = (f32[48,128]{1,0:T(8,128)S(1)}, f32[48,128]{1,0:T(8,128)S(1)}, u32[]{:S(2)}, u32[]{:S(2)}) collective-permute-start(f32[48,128]{1,0:T(8,128)S(1)} %add.370), channel_id=1, source_target_pairs={{0,32},{16,48},{32,0},{48,16},{64,96},{80,112},{96,64},{112,80},{1... | collective-permute-start | bytes 73736 | tf_op jit(solution)/shard_map/x_other/ppermute | solution.py:16
  155.4 10.6 %collective-permute-done.27 = f32[48,128]{1,0:T(8,128)S(1)} collective-permute-done((f32[48,128]{1,0:T(8,128)S(1)}, f32[48,128]{1,0:T(8,128)S(1)}, u32[]{:S(2)}, u32[]{:S(2)}) %collective-permute-start.27) | collective-permute-done | bytes 24608 | tf_op jit(solution)/shard_map/x_other/ppermute | solution.py:16
  166.3 1.3 collective-permute-start.28
  167.6 0.8 collective-permute-start.29
  168.4 0.8 collective-permute-start.30
  169.2 1.3 collective-permute-start.31
  170.6 13.6 %collective-permute-done.31 = f32[48,128]{1,0:T(8,128)S(1)} collective-permute-done((f32[48,128]{1,0:T(8,128)S(1)}, f32[48,128]{1,0:T(8,128)S(1)}, u32[]{:S(2)}, u32[]{:S(2)}) %collective-permute-start.31) | collective-permute-done | bytes 24608 | tf_op jit(solution)/shard_map/x_own/ppermute | solution.py:16
  184.2 0.6 fusion.27
  184.8 0.4 fusion.5
  185.2 1.4 copy.8
  186.6 1.3 fusion.18
  188.0 2.1 %fusion.16 = bf16[32,6144]{1,0:T(8,128)(2,1)} fusion(bf16[32,6144]{1,0:T(8,128)(2,1)S(1)} %copy-done.29, bf16[32,6144]{1,0:T(8,128)(2,1)} %reduce-scatter.2.cloned.1.call-done, bf16[32,6144]{1,0:T(8,128)(2,1)S(1)} %copy-done.33, f32[32]{0:T(128)S(1)} %get-tuple-element.119, f32[32]{0:T(128)S(1)} %get-tuple-element.120, f32[6144]{0:T(1024)S(1)} %copy-done.32, ...), kind=kLoop, calls=%fused_computation.22 | loop fusion | flops 2359296 | bytes 1597952 | tf_op jit(solution)/shard_map/input_gradient/convert_element_type | solution.py:374
  (124 shorter events, 2.6 us)
Async XLA Ops:
  7.2 23.9 %copy-start.4 = (bf16[512,768]{1,0:T(8,128)(2,1)S(1)}, bf16[512,768]{1,0:T(8,128)(2,1)}, u32[]{:S(2)}) copy-start(bf16[512,768]{1,0:T(8,128)(2,1)} %refs_6_.9) | copy-start | bytes 2359300
  7.2 179.4 %reduce-scatter.2.cloned.1.call-start = ((), (), s32[]{:S(2)}) async-start(), calls=%async_computation.1 | async-start | bytes 6684672 | tf_op jit(solution)/shard_map/scatter/reduce_scatter | solution.py:310
  10.9 28.0 %copy-start.5 = (bf16[32,6144]{1,0:T(8,128)(2,1)}, bf16[32,6144]{1,0:T(8,128)(2,1)S(1)}, u32[]{:S(2)}) copy-start(bf16[32,6144]{1,0:T(8,128)(2,1)S(1)} %fusion.11.refs_0_) | copy-start | bytes 1179652
  10.9 15.2 %collective-permute-start.1 = (bf16[32,6144]{1,0:T(8,128)(2,1)S(1)}, bf16[32,6144]{1,0:T(8,128)(2,1)}, u32[]{:S(2)}, u32[]{:S(2)}) collective-permute-start(bf16[32,6144]{1,0:T(8,128)(2,1)S(1)} %fusion.11.refs_0_), channel_id=1, source_target_pairs={{0,1},{1,2},{2,3},{3,4},{4,5},{5,6},{6,7},{7,0},{8,9},{9,10},{10,1... | collective-permute-start | bytes 1179656 | tf_op jit(solution)/shard_map/gather/ppermute | solution.py:16
  12.9 13.2 %collective-permute-start = (bf16[32,6144]{1,0:T(8,128)(2,1)S(1)}, bf16[32,6144]{1,0:T(8,128)(2,1)S(1)}, u32[]{:S(2)}, u32[]{:S(2)}) collective-permute-start(bf16[32,6144]{1,0:T(8,128)(2,1)S(1)} %fusion.11.refs_0_), channel_id=1, source_target_pairs={{0,7},{1,0},{2,1},{3,2},{4,3},{5,4},{6,5},{7,6},{8,15},{9,8},{10,9... | collective-permute-start | bytes 1179656 | tf_op jit(solution)/shard_map/gather/ppermute | solution.py:16
  17.0 14.1 %collective-permute-start.4 = (bf16[32,6144]{1,0:T(8,128)(2,1)S(1)}, bf16[32,6144]{1,0:T(8,128)(2,1)S(1)}, u32[]{:S(2)}, u32[]{:S(2)}) collective-permute-start(bf16[32,6144]{1,0:T(8,128)(2,1)S(1)} %fusion.11.refs_0_), channel_id=1, source_target_pairs={{0,8},{1,9},{2,10},{3,11},{4,12},{5,13},{6,14},{7,15},{8,0},{9,1},... | collective-permute-start | bytes 1179656 | tf_op jit(solution)/shard_map/gather/ppermute | solution.py:16
  26.1 12.9 %copy-start.18 = (bf16[32,6144]{1,0:T(8,128)(2,1)}, bf16[32,6144]{1,0:T(8,128)(2,1)S(1)}, u32[]{:S(2)}) copy-start(bf16[32,6144]{1,0:T(8,128)(2,1)S(1)} %collective-permute-done.refs_1_) | copy-start | bytes 1179652
  26.1 13.6 %collective-permute-start.3 = (bf16[32,6144]{1,0:T(8,128)(2,1)}, bf16[32,6144]{1,0:T(8,128)(2,1)S(1)}, u32[]{:S(2)}, u32[]{:S(2)}) collective-permute-start(bf16[32,6144]{1,0:T(8,128)(2,1)} %collective-permute-done.1.refs_2_), channel_id=1, source_target_pairs={{0,1},{1,2},{2,3},{3,4},{4,5},{5,6},{6,7},{7,0},{8,9},{9,10},{10,1... | collective-permute-start | bytes 1179656 | tf_op jit(solution)/shard_map/gather/ppermute | solution.py:16
  26.1 13.6 %collective-permute-start.2 = (bf16[32,6144]{1,0:T(8,128)(2,1)S(1)}, bf16[32,6144]{1,0:T(8,128)(2,1)S(1)}, u32[]{:S(2)}, u32[]{:S(2)}) collective-permute-start(bf16[32,6144]{1,0:T(8,128)(2,1)S(1)} %collective-permute-done.refs_1_), channel_id=1, source_target_pairs={{0,7},{1,0},{2,1},{3,2},{4,3},{5,4},{6,5},{7,6},{8,15},{9,8},{10,9... | collective-permute-start | bytes 1179656 | tf_op jit(solution)/shard_map/gather/ppermute | solution.py:16
  29.4 14.1 %collective-permute-start.7 = (bf16[32,6144]{1,0:T(8,128)(2,1)S(1)}, bf16[32,6144]{1,0:T(8,128)(2,1)S(1)}, u32[]{:S(2)}, u32[]{:S(2)}) collective-permute-start(bf16[32,6144]{1,0:T(8,128)(2,1)S(1)} %collective-permute-done.refs_1_), channel_id=1, source_target_pairs={{0,8},{1,9},{2,10},{3,11},{4,12},{5,13},{6,14},{7,15},{8,0},{9,1},... | collective-permute-start | bytes 1179656 | tf_op jit(solution)/shard_map/gather/ppermute | solution.py:16
  31.0 3.7 %copy-start = (bf16[6144,768]{1,0:T(8,128)(2,1)S(1)}, bf16[6144,768]{1,0:T(8,128)(2,1)}, u32[]{:S(2)}) copy-start(bf16[6144,768]{1,0:T(8,128)(2,1)} %refs_3_.7) | copy-start | bytes 28311556
  34.7 4.3 %copy-start.19 = (bf16[32,6144]{1,0:T(8,128)(2,1)}, bf16[32,6144]{1,0:T(8,128)(2,1)S(1)}, u32[]{:S(2)}) copy-start(bf16[32,6144]{1,0:T(8,128)(2,1)S(1)} %collective-permute-done.4.refs_3_) | copy-start | bytes 1179652
  39.7 14.3 %copy-start.6 = (bf16[32,6144]{1,0:T(8,128)(2,1)}, bf16[32,6144]{1,0:T(8,128)(2,1)S(1)}, u32[]{:S(2)}) copy-start(bf16[32,6144]{1,0:T(8,128)(2,1)S(1)} %collective-permute-done.3.refs_1_.refs_5_) | copy-start | bytes 1179652
  39.7 10.6 %copy-start.7 = (bf16[32,6144]{1,0:T(8,128)(2,1)}, bf16[32,6144]{1,0:T(8,128)(2,1)S(1)}, u32[]{:S(2)}) copy-start(bf16[32,6144]{1,0:T(8,128)(2,1)S(1)} %collective-permute-done.2.refs_0_.refs_4_) | copy-start | bytes 1179652
  39.7 11.3 %collective-permute-start.6 = (bf16[32,6144]{1,0:T(8,128)(2,1)S(1)}, bf16[32,6144]{1,0:T(8,128)(2,1)S(1)}, u32[]{:S(2)}, u32[]{:S(2)}) collective-permute-start(bf16[32,6144]{1,0:T(8,128)(2,1)S(1)} %collective-permute-done.3.refs_1_.refs_5_), channel_id=1, source_target_pairs={{0,1},{1,2},{2,3},{3,4},{4,5},{5,6},{6,7},{7,0},{8,9},{9,10},{10,1... | collective-permute-start | bytes 1179656 | tf_op jit(solution)/shard_map/gather/ppermute | solution.py:16
  39.8 11.2 %collective-permute-start.5 = (bf16[32,6144]{1,0:T(8,128)(2,1)S(1)}, bf16[32,6144]{1,0:T(8,128)(2,1)S(1)}, u32[]{:S(2)}, u32[]{:S(2)}) collective-permute-start(bf16[32,6144]{1,0:T(8,128)(2,1)S(1)} %collective-permute-done.2.refs_0_.refs_4_), channel_id=1, source_target_pairs={{0,7},{1,0},{2,1},{3,2},{4,3},{5,4},{6,5},{7,6},{8,15},{9,8},{10,9... | collective-permute-start | bytes 1179656 | tf_op jit(solution)/shard_map/gather/ppermute | solution.py:16
  43.0 8.9 %collective-permute-start.8 = (bf16[32,6144]{1,0:T(8,128)(2,1)S(1)}, bf16[32,6144]{1,0:T(8,128)(2,1)S(1)}, u32[]{:S(2)}, u32[]{:S(2)}) collective-permute-start(bf16[32,6144]{1,0:T(8,128)(2,1)S(1)} %collective-permute-done.2.refs_0_.refs_4_), channel_id=1, source_target_pairs={{0,8},{1,9},{2,10},{3,11},{4,12},{5,13},{6,14},{7,15},{8,0},{9,1},... | collective-permute-start | bytes 1179656 | tf_op jit(solution)/shard_map/gather/ppermute | solution.py:16
  43.5 3.7 %copy-start.1 = (bf16[6144,768]{1,0:T(8,128)(2,1)S(1)}, bf16[6144,768]{1,0:T(8,128)(2,1)}, u32[]{:S(2)}) copy-start(bf16[6144,768]{1,0:T(8,128)(2,1)} %refs_3_.7) | copy-start | bytes 28311556
  51.0 10.6 %copy-start.9 = (bf16[32,6144]{1,0:T(8,128)(2,1)}, bf16[32,6144]{1,0:T(8,128)(2,1)S(1)}, u32[]{:S(2)}) copy-start(bf16[32,6144]{1,0:T(8,128)(2,1)S(1)} %collective-permute-done.6.refs_1_.refs_8_) | copy-start | bytes 1179652
  51.0 10.6 %copy-start.10 = (bf16[32,6144]{1,0:T(8,128)(2,1)}, bf16[32,6144]{1,0:T(8,128)(2,1)S(1)}, u32[]{:S(2)}) copy-start(bf16[32,6144]{1,0:T(8,128)(2,1)S(1)} %collective-permute-done.5.refs_0_.refs_7_) | copy-start | bytes 1179652
  51.9 9.6 %copy-start.11 = (bf16[32,6144]{1,0:T(8,128)(2,1)}, bf16[32,6144]{1,0:T(8,128)(2,1)S(1)}, u32[]{:S(2)}) copy-start(bf16[32,6144]{1,0:T(8,128)(2,1)S(1)} %collective-permute-done.8.refs_2_.refs_9_) | copy-start | bytes 1179652
  51.9 10.3 %collective-permute-start.9 = (bf16[32,6144]{1,0:T(8,128)(2,1)S(1)}, bf16[32,6144]{1,0:T(8,128)(2,1)S(1)}, u32[]{:S(2)}, u32[]{:S(2)}) collective-permute-start(bf16[32,6144]{1,0:T(8,128)(2,1)S(1)} %collective-permute-done.8.refs_2_.refs_9_), channel_id=1, source_target_pairs={{0,7},{1,0},{2,1},{3,2},{4,3},{5,4},{6,5},{7,6},{8,15},{9,8},{10,9... | collective-permute-start | bytes 1179656 | tf_op jit(solution)/shard_map/gather/ppermute | solution.py:16
  53.5 9.2 %collective-permute-start.10 = (bf16[32,6144]{1,0:T(8,128)(2,1)S(1)}, bf16[32,6144]{1,0:T(8,128)(2,1)S(1)}, u32[]{:S(2)}, u32[]{:S(2)}) collective-permute-start(bf16[32,6144]{1,0:T(8,128)(2,1)S(1)} %collective-permute-done.6.refs_1_.refs_8_), channel_id=1, source_target_pairs={{0,1},{1,2},{2,3},{3,4},{4,5},{5,6},{6,7},{7,0},{8,9},{9,10},{10,1... | collective-permute-start | bytes 1179656 | tf_op jit(solution)/shard_map/gather/ppermute | solution.py:16
  53.9 8.7 %collective-permute-start.12 = (bf16[32,6144]{1,0:T(8,128)(2,1)S(1)}, bf16[32,6144]{1,0:T(8,128)(2,1)S(1)}, u32[]{:S(2)}, u32[]{:S(2)}) collective-permute-start(bf16[32,6144]{1,0:T(8,128)(2,1)S(1)} %collective-permute-done.3.refs_1_.refs_5_), channel_id=1, source_target_pairs={{0,8},{1,9},{2,10},{3,11},{4,12},{5,13},{6,14},{7,15},{8,0},{9,1},... | collective-permute-start | bytes 1179656 | tf_op jit(solution)/shard_map/gather/ppermute | solution.py:16
  54.8 3.7 %copy-start.2 = (bf16[6144,768]{1,0:T(8,128)(2,1)S(1)}, bf16[6144,768]{1,0:T(8,128)(2,1)}, u32[]{:S(2)}) copy-start(bf16[6144,768]{1,0:T(8,128)(2,1)} %refs_3_.7) | copy-start | bytes 28311556
  62.3 11.6 %copy-start.12 = (bf16[32,6144]{1,0:T(8,128)(2,1)}, bf16[32,6144]{1,0:T(8,128)(2,1)S(1)}, u32[]{:S(2)}) copy-start(bf16[32,6144]{1,0:T(8,128)(2,1)S(1)} %collective-permute-done.9.refs_0_.refs_10_) | copy-start | bytes 1179652
  62.7 11.2 %copy-start.13 = (bf16[32,6144]{1,0:T(8,128)(2,1)}, bf16[32,6144]{1,0:T(8,128)(2,1)S(1)}, u32[]{:S(2)}) copy-start(bf16[32,6144]{1,0:T(8,128)(2,1)S(1)} %collective-permute-done.10.refs_1_.refs_11_) | copy-start | bytes 1179652
  62.7 11.2 %copy-start.14 = (bf16[32,6144]{1,0:T(8,128)(2,1)}, bf16[32,6144]{1,0:T(8,128)(2,1)S(1)}, u32[]{:S(2)}) copy-start(bf16[32,6144]{1,0:T(8,128)(2,1)S(1)} %collective-permute-done.12.refs_2_.refs_12_) | copy-start | bytes 1179652
  62.7 11.3 %collective-permute-start.13 = (bf16[32,6144]{1,0:T(8,128)(2,1)S(1)}, bf16[32,6144]{1,0:T(8,128)(2,1)S(1)}, u32[]{:S(2)}, u32[]{:S(2)}) collective-permute-start(bf16[32,6144]{1,0:T(8,128)(2,1)S(1)} %collective-permute-done.12.refs_2_.refs_12_), channel_id=1, source_target_pairs={{0,1},{1,2},{2,3},{3,4},{4,5},{5,6},{6,7},{7,0},{8,9},{9,10},{10,1... | collective-permute-start | bytes 1179656 | tf_op jit(solution)/shard_map/gather/ppermute | solution.py:16
  62.8 11.2 %collective-permute-start.11 = (bf16[32,6144]{1,0:T(8,128)(2,1)S(1)}, bf16[32,6144]{1,0:T(8,128)(2,1)S(1)}, u32[]{:S(2)}, u32[]{:S(2)}) collective-permute-start(bf16[32,6144]{1,0:T(8,128)(2,1)S(1)} %collective-permute-done.9.refs_0_.refs_10_), channel_id=1, source_target_pairs={{0,7},{1,0},{2,1},{3,2},{4,3},{5,4},{6,5},{7,6},{8,15},{9,8},{10,9... | collective-permute-start | bytes 1179656 | tf_op jit(solution)/shard_map/gather/ppermute | solution.py:16
  66.0 8.0 %collective-permute-start.14 = (bf16[32,6144]{1,0:T(8,128)(2,1)}, bf16[32,6144]{1,0:T(8,128)(2,1)S(1)}, u32[]{:S(2)}, u32[]{:S(2)}) collective-permute-start(bf16[32,6144]{1,0:T(8,128)(2,1)} %collective-permute-done.1.refs_2_), channel_id=1, source_target_pairs={{0,8},{1,9},{2,10},{3,11},{4,12},{5,13},{6,14},{7,15},{8,0},{9,1},... | collective-permute-start | bytes 1179656 | tf_op jit(solution)/shard_map/gather/ppermute | solution.py:16
  67.0 10.1 %copy-start.28 = (s32[16]{0:T(128)}, s32[16]{0:T(128)S(1)}, u32[]{:S(2)}) copy-start(s32[16]{0:T(128)S(1)} %stack.122.slots) | copy-start | bytes 196
  67.1 3.7 %copy-start.3 = (bf16[6144,768]{1,0:T(8,128)(2,1)S(1)}, bf16[6144,768]{1,0:T(8,128)(2,1)}, u32[]{:S(2)}) copy-start(bf16[6144,768]{1,0:T(8,128)(2,1)} %refs_3_.7) | copy-start | bytes 28311556
  70.8 8.2 %slice-start = ((s8[9437184]{0:T(1024)(128)(4,1)}), s8[4194304]{0:T(1024)(128)(4,1)S(1)}, s32[]{:S(2)}) async-start(s8[9437184]{0:T(1024)(128)(4,1)} %bitcast.63), calls=%async_computation.2 | async-start | bytes 8388608
  70.8 8.2 %slice-start.1 = ((s8[9437184]{0:T(1024)(128)(4,1)}), s8[4194304]{0:T(1024)(128)(4,1)S(1)}, s32[]{:S(2)}) async-start(s8[9437184]{0:T(1024)(128)(4,1)} %bitcast.63), calls=%async_computation.3 | async-start | bytes 8388608
  73.9 3.2 %copy-start.26 = (bf16[96,768]{1,0:T(8,128)(2,1)}, bf16[96,768]{1,0:T(8,128)(2,1)S(1)}, u32[]{:S(2)}) copy-start(bf16[96,768]{1,0:T(8,128)(2,1)S(1)} %forward.8.refs_3_.refs_19_) | copy-start | bytes 442372
  73.9 3.2 %copy-start.21 = (bf16[128,768]{1,0:T(8,128)(2,1)S(1)}, bf16[128,768]{1,0:T(8,128)(2,1)}, u32[]{:S(2)}) copy-start(bf16[128,768]{1,0:T(8,128)(2,1)} %copy-done.20) | copy-start | bytes 589828
  73.9 3.2 %copy-start.23 = (bf16[96,768]{1,0:T(8,128)(2,1)S(1)}, bf16[96,768]{1,0:T(8,128)(2,1)}, u32[]{:S(2)}) copy-start(bf16[96,768]{1,0:T(8,128)(2,1)} %copy-done.22) | copy-start | bytes 442372
  74.0 3.2 %copy-start.25 = (bf16[96,768]{1,0:T(8,128)(2,1)S(1)}, bf16[96,768]{1,0:T(8,128)(2,1)}, u32[]{:S(2)}) copy-start(bf16[96,768]{1,0:T(8,128)(2,1)} %copy-done.24) | copy-start | bytes 442372
  74.0 5.1 %slice-start.2 = ((s8[9437184]{0:T(1024)(128)(4,1)}), s8[1048576]{0:T(1024)(128)(4,1)S(1)}, s32[]{:S(2)}) async-start(s8[9437184]{0:T(1024)(128)(4,1)} %bitcast.63), calls=%async_computation.4 | async-start | bytes 2097152
  74.0 3.2 %copy-start.15 = (bf16[32,6144]{1,0:T(8,128)(2,1)}, bf16[32,6144]{1,0:T(8,128)(2,1)S(1)}, u32[]{:S(2)}) copy-start(bf16[32,6144]{1,0:T(8,128)(2,1)S(1)} %collective-permute-done.13.refs_1_.refs_14_) | copy-start | bytes 1179652
  74.0 3.1 %copy-start.16 = (bf16[32,6144]{1,0:T(8,128)(2,1)}, bf16[32,6144]{1,0:T(8,128)(2,1)S(1)}, u32[]{:S(2)}) copy-start(bf16[32,6144]{1,0:T(8,128)(2,1)S(1)} %collective-permute-done.11.refs_0_.refs_13_) | copy-start | bytes 1179652
  77.2 8.9 %copy-start.27 = (bf16[96,768]{1,0:T(8,128)(2,1)}, bf16[96,768]{1,0:T(8,128)(2,1)S(1)}, u32[]{:S(2)}) copy-start(bf16[96,768]{1,0:T(8,128)(2,1)S(1)} %forward.9.refs_4_.refs_20_) | copy-start | bytes 442372
  101.6 1.3 collective-permute-start.15
  102.9 11.4 %copy-start.34 = (bf16[2,768,384]{2,1,0:T(8,128)(2,1)S(1)}, bf16[2,768,384]{2,1,0:T(8,128)(2,1)}, u32[]{:S(2)}) copy-start(bf16[2,768,384]{2,1,0:T(8,128)(2,1)} %get-tuple-element.81) | copy-start | bytes 3538948
  102.9 14.3 %copy-start.31 = (bf16[2,768,384]{2,1,0:T(8,128)(2,1)S(1)}, bf16[2,768,384]{2,1,0:T(8,128)(2,1)}, u32[]{:S(2)}) copy-start(bf16[2,768,384]{2,1,0:T(8,128)(2,1)} %get-tuple-element.80) | copy-start | bytes 3538948
  102.9 11.4 %collective-permute-start.16 = (f32[48,128]{1,0:T(8,128)S(1)}, f32[48,128]{1,0:T(8,128)S(1)}, u32[]{:S(2)}, u32[]{:S(2)}) collective-permute-start(f32[48,128]{1,0:T(8,128)S(1)} %add.350), channel_id=1, source_target_pairs={{0,1},{1,0},{2,3},{3,2},{4,5},{5,4},{6,7},{7,6},{8,9},{9,8},{10,11... | collective-permute-start | bytes 73736 | tf_op jit(solution)/shard_map/weights/ppermute | solution.py:16
  114.3 2.9 %collective-permute-start.17 = (bf16[2,768,384]{2,1,0:T(8,128)(2,1)S(1)}, bf16[2,768,384]{2,1,0:T(8,128)(2,1)S(1)}, u32[]{:S(2)}, u32[]{:S(2)}) collective-permute-start(bf16[2,768,384]{2,1,0:T(8,128)(2,1)S(1)} %copy-done.34), channel_id=1, source_target_pairs={{0,16},{16,0},{32,48},{48,32},{64,80},{80,64},{96,112},{112,96},{1... | collective-permute-start | bytes 3538952 | tf_op jit(solution)/shard_map/core_far/ppermute | solution.py:16
  117.3 21.5 %copy-start.30 = (bf16[6,768,384]{2,1,0:T(8,128)(2,1)S(1)}, bf16[6,768,384]{2,1,0:T(8,128)(2,1)}, u32[]{:S(2)}) copy-start(bf16[6,768,384]{2,1,0:T(8,128)(2,1)} %get-tuple-element.79) | copy-start | bytes 10616836
  117.6 21.1 %collective-permute-start.20 = (bf16[6,768,384]{2,1,0:T(8,128)(2,1)}, bf16[6,768,384]{2,1,0:T(8,128)(2,1)S(1)}, u32[]{:S(2)}, u32[]{:S(2)}) collective-permute-start(bf16[6,768,384]{2,1,0:T(8,128)(2,1)} %get-tuple-element.85), channel_id=1, source_target_pairs={{0,16},{16,0},{32,48},{48,32},{64,80},{80,64},{96,112},{112,96},{1... | collective-permute-start | bytes 10616840 | tf_op jit(solution)/shard_map/x_far/ppermute | solution.py:16
  117.9 20.8 %collective-permute-start.19 = (bf16[2,384,384]{2,1,0:T(8,128)(2,1)S(1)}, bf16[2,384,384]{2,1,0:T(8,128)(2,1)S(1)}, u32[]{:S(2)}, u32[]{:S(2)}) collective-permute-start(bf16[2,384,384]{2,1,0:T(8,128)(2,1)S(1)} %get-tuple-element.117), channel_id=1, source_target_pairs={{0,192},{16,208},{32,224},{48,240},{64,0},{80,16},{96,32},{112,48}... | collective-permute-start | bytes 1769480 | tf_op jit(solution)/shard_map/x_far/ppermute | solution.py:16
  118.6 20.1 %collective-permute-start.18 = (bf16[2,384,384]{2,1,0:T(8,128)(2,1)S(1)}, bf16[2,384,384]{2,1,0:T(8,128)(2,1)S(1)}, u32[]{:S(2)}, u32[]{:S(2)}) collective-permute-start(bf16[2,384,384]{2,1,0:T(8,128)(2,1)S(1)} %get-tuple-element.118), channel_id=1, source_target_pairs={{0,64},{16,80},{32,96},{48,112},{64,128},{80,144},{96,160},{112,17... | collective-permute-start | bytes 1769480 | tf_op jit(solution)/shard_map/x_far/ppermute | solution.py:16
  120.1 5.7 %collective-permute-start.21 = (f32[48,128]{1,0:T(8,128)S(1)}, f32[48,128]{1,0:T(8,128)S(1)}, u32[]{:S(2)}, u32[]{:S(2)}) collective-permute-start(f32[48,128]{1,0:T(8,128)S(1)} %add.351), channel_id=1, source_target_pairs={{0,2},{1,3},{2,0},{3,1},{4,6},{5,7},{6,4},{7,5},{8,10},{9,11},{10,... | collective-permute-start | bytes 73736 | tf_op jit(solution)/shard_map/x_far/ppermute | solution.py:16
  125.8 8.4 %collective-permute-start.22 = (f32[48,128]{1,0:T(8,128)S(1)}, f32[48,128]{1,0:T(8,128)S(1)}, u32[]{:S(2)}, u32[]{:S(2)}) collective-permute-start(f32[48,128]{1,0:T(8,128)S(1)} %add.353), channel_id=1, source_target_pairs={{0,4},{1,5},{2,6},{3,7},{4,0},{5,1},{6,2},{7,3},{8,12},{9,13},{10,... | collective-permute-start | bytes 73736 | tf_op jit(solution)/shard_map/x_far/ppermute | solution.py:16
  134.2 4.4 %collective-permute-start.23 = (f32[48,128]{1,0:T(8,128)S(1)}, f32[48,128]{1,0:T(8,128)S(1)}, u32[]{:S(2)}, u32[]{:S(2)}) collective-permute-start(f32[48,128]{1,0:T(8,128)S(1)} %add.354), channel_id=1, source_target_pairs={{0,64},{16,80},{32,96},{48,112},{64,0},{80,16},{96,32},{112,48},{1... | collective-permute-start | bytes 73736 | tf_op jit(solution)/shard_map/x_far/ppermute | solution.py:16
  139.7 26.3 %collective-permute-start.24 = (bf16[768,384]{1,0:T(8,128)(2,1)S(1)}, bf16[768,384]{1,0:T(8,128)(2,1)S(1)}, u32[]{:S(2)}, u32[]{:S(2)}) collective-permute-start(bf16[768,384]{1,0:T(8,128)(2,1)S(1)} %get-tuple-element.91), channel_id=1, source_target_pairs={{0,64},{16,80},{32,96},{48,112},{64,128},{80,144},{96,160},{112,17... | collective-permute-start | bytes 1769480 | tf_op jit(solution)/shard_map/x_other/ppermute | solution.py:16
  141.8 24.2 %collective-permute-start.25 = (bf16[768,384]{1,0:T(8,128)(2,1)S(1)}, bf16[768,384]{1,0:T(8,128)(2,1)S(1)}, u32[]{:S(2)}, u32[]{:S(2)}) collective-permute-start(bf16[768,384]{1,0:T(8,128)(2,1)S(1)} %get-tuple-element.92), channel_id=1, source_target_pairs={{0,192},{16,208},{32,224},{48,240},{64,0},{80,16},{96,32},{112,48}... | collective-permute-start | bytes 1769480 | tf_op jit(solution)/shard_map/x_other/ppermute | solution.py:16
  141.8 10.5 %collective-permute-start.26 = (f32[48,128]{1,0:T(8,128)S(1)}, f32[48,128]{1,0:T(8,128)S(1)}, u32[]{:S(2)}, u32[]{:S(2)}) collective-permute-start(f32[48,128]{1,0:T(8,128)S(1)} %add.355), channel_id=1, source_target_pairs={{0,128},{16,144},{32,160},{48,176},{64,192},{80,208},{96,224},{112... | collective-permute-start | bytes 73736 | tf_op jit(solution)/shard_map/x_other/ppermute | solution.py:16
  152.3 13.7 %collective-permute-start.27 = (f32[48,128]{1,0:T(8,128)S(1)}, f32[48,128]{1,0:T(8,128)S(1)}, u32[]{:S(2)}, u32[]{:S(2)}) collective-permute-start(f32[48,128]{1,0:T(8,128)S(1)} %add.370), channel_id=1, source_target_pairs={{0,32},{16,48},{32,0},{48,16},{64,96},{80,112},{96,64},{112,80},{1... | collective-permute-start | bytes 73736 | tf_op jit(solution)/shard_map/x_other/ppermute | solution.py:16
  166.0 18.2 %copy-start.32 = (f32[6144]{0:T(1024)S(1)}, f32[6144]{0:T(1024)}, u32[]{:S(2)}) copy-start(f32[6144]{0:T(1024)} %param.6) | copy-start | bytes 73732
  166.3 18.5 %collective-permute-start.28 = (bf16[768,384]{1,0:T(8,128)(2,1)S(1)}, bf16[768,384]{1,0:T(8,128)(2,1)S(1)}, u32[]{:S(2)}, u32[]{:S(2)}) collective-permute-start(bf16[768,384]{1,0:T(8,128)(2,1)S(1)} %get-tuple-element.99), channel_id=1, source_target_pairs={{0,64},{16,80},{32,96},{48,112},{64,128},{80,144},{96,160},{112,17... | collective-permute-start | bytes 1769480 | tf_op jit(solution)/shard_map/x_own/ppermute | solution.py:16
  167.6 17.2 %collective-permute-start.29 = (bf16[768,384]{1,0:T(8,128)(2,1)S(1)}, bf16[768,384]{1,0:T(8,128)(2,1)S(1)}, u32[]{:S(2)}, u32[]{:S(2)}) collective-permute-start(bf16[768,384]{1,0:T(8,128)(2,1)S(1)} %get-tuple-element.100), channel_id=1, source_target_pairs={{0,192},{16,208},{32,224},{48,240},{64,0},{80,16},{96,32},{112,48}... | collective-permute-start | bytes 1769480 | tf_op jit(solution)/shard_map/x_own/ppermute | solution.py:16
  168.4 16.4 %collective-permute-start.30 = (bf16[768,384]{1,0:T(8,128)(2,1)S(1)}, bf16[768,384]{1,0:T(8,128)(2,1)S(1)}, u32[]{:S(2)}, u32[]{:S(2)}) collective-permute-start(bf16[768,384]{1,0:T(8,128)(2,1)S(1)} %fusion.1), channel_id=1, source_target_pairs={{0,32},{16,48},{32,0},{48,16},{64,96},{80,112},{96,64},{112,80},{1... | collective-permute-start | bytes 1769480 | tf_op jit(solution)/shard_map/x_own/ppermute | solution.py:16
  169.2 14.9 %collective-permute-start.31 = (f32[48,128]{1,0:T(8,128)S(1)}, f32[48,128]{1,0:T(8,128)S(1)}, u32[]{:S(2)}, u32[]{:S(2)}) collective-permute-start(f32[48,128]{1,0:T(8,128)S(1)} %add.371), channel_id=1, source_target_pairs={{0,8},{1,9},{2,10},{3,11},{4,12},{5,13},{6,14},{7,15},{8,0},{9,1},... | collective-permute-start | bytes 73736 | tf_op jit(solution)/shard_map/x_own/ppermute | solution.py:16
  (7 other events, 12.4 us)
Sparse Core Ops, SparseCore 0:
  86.2 87.2 reduce-scatter.1
where the time goes:
time: 198 us; the launch traced here: 197 us
  waiting for transfers between devices  54.4 us (27%)
  starting transfers between devices  47 us (24%)
  Pallas kernels  42.8 us (22%)
  local copies, waits for them, and re-layouts  18.5 us (9%)
  between operations  14.8 us (7%)
  other arithmetic  12.4 us (6%)
  matrix products  7.02 us (4%)
    ppermute x32, waiting for transfers between devices, ppermute(): return lax.ppermute(value, axis, [(i, target(i)) for i in range(16)])  54.4 us
    ppermute x32, starting transfers between devices, ppermute(): return lax.ppermute(value, axis, [(i, target(i)) for i in range(16)])  47 us
    unnamed x77, local copies, waits for them, and re-layouts  18.2 us
    pallas_call x2, Pallas kernels, weight_terms(): pl.pallas_call(weight_kernel, grid_spec=pltpu.PrefetchScalarGridSpec(num_...  17.2 us
    pallas_call x5, Pallas kernels, forward(): pl.pallas_call(forward_kernel, grid_spec=pltpu.PrefetchScalarGridSpec(num...  16.5 us
    pallas_call x1, Pallas kernels, scale_sum(): pl.pallas_call(scale_kernel, grid_spec=pltpu.PrefetchScalarGridSpec(num_s...  7.34 us
    dot_general x1, matrix products, backward(): lax.dot_general(dpre, w_in, (((1,), (1,)), ((), ())), preferred_element_t...  7.02 us
  transfers between devices with their start and end apart: 33, of which 11 were waited for; matrix products, arithmetic and copies ran while one was open for 3% of the time, Pallas kernels for 19%

commit v1 on v0

--- a/solution.py
+++ b/solution.py
@@ -275,6 +275,8 @@
         ]
         return jnp.stack(places).astype(jnp.int32)
 
+    place = jnp.stack([yh_at, c_at]).astype(jnp.int32)
+    order = jnp.stack([(x_at + k) % 4 for k in (2, 1, 3, 0)]).astype(jnp.int32)
     got = {("A", 0): normed_output}
     rights = []
 
@@ -285,6 +287,8 @@
         for at, moves in enumerate(MOVES):
             for key, move, source in moves:
                 got[key] = move(got[source])
+            if at == 2:
+                got["A", 3], order, place = together(got["A", 3], order, place)
             along_z = [key for key, move, _ in moves if move is not swap_y]
             held = [got[key] for key in along_z]
             if at >= 1:
@@ -309,8 +313,6 @@
     with jax.named_scope("scatter"):
         normed_gradient = lax.psum_scatter(product, "tensor", scatter_dimension=0, tiled=True).astype(F32)
 
-    place = jnp.stack([yh_at, c_at]).astype(jnp.int32)
-    order = jnp.stack([(x_at + k) % 4 for k in (2, 1, 3, 0)]).astype(jnp.int32)
     half = w_in.shape[1] // 2
 
     def hop(total, axis, bit):
@@ -328,7 +330,7 @@
         total = jnp.sum(sums, axis=0).reshape(48, 128)
         far_mine, far_theirs, second, total = together(far_mine, far_theirs, second, total)
         mine, theirs = weight_terms(second, place, blocks, rights)
-        total = hop(hop(total, "dp", 1), "tensor", 1)
+        total = hop(hop(total, "dp", 1), "dp", 4)
         far_mine, far_theirs, mine, theirs, total = together(far_mine, far_theirs, mine, theirs, total)
 
     with jax.named_scope("core_far"):
@@ -338,7 +340,7 @@
     with jax.named_scope("x_far"):
         far_up, far_down = to_x(far[:, :half], 1), to_x(far[:, half:], -1)
         theirs = swap_core(theirs)
-        total = hop(hop(hop(total, "tensor", 2), "tensor", 4), "dp", 4)
+        total = hop(total, "dp", 2)
         far_up, far_down, theirs, total = together(far_up, far_down, theirs, total)
 
     with jax.named_scope("x_other"):
@@ -346,7 +348,7 @@
         up_other, down_other, total = together(up_other, down_other, total)
         up_moved, down_moved = to_x(up_other, 1), to_x(down_other, -1)
         up_own, down_own = moving(mine, theirs, far_up[1:], 1, 1), moving(mine, theirs, far_down[1:], 3, -1)
-        total = hop(hop(total, "dp", 8), "dp", 2)
+        total = hop(hop(hop(total, "tensor", 1), "tensor", 2), "tensor", 4)
         up_moved, down_moved, up_own, down_own, total = together(
             up_moved, down_moved, up_own, down_own, total
         )
@@ -360,8 +362,7 @@
         for value in (up_moved, down_moved, from_y):
             own = own + value.astype(F32)
         grad_w = (own / 16).T
-        total = hop(total, "tensor", 8)
-        scale_gradient = total.reshape(-1) / gain / 16
+        last = ppermute(total, "dp", lambda i: i ^ 8)
 
     with jax.named_scope("input_gradient"):
         scaled_gradient = normed_gradient * gain
@@ -372,6 +373,9 @@
             + inverse_deviation
             * (scaled_gradient - first_average - standardized_input * second_average)
         ).astype(BF16)
+    with jax.named_scope("scale_gradient"):
+        last, block_input_gradient = together(last, block_input_gradient)
+        scale_gradient = hop(total + last, "tensor", 8).reshape(-1) / gain / 16
     return (block_input_gradient, grad_w, scale_gradient)
 
 

time: 198 us -> 195 us (0.985)
  starting transfers between devices: 47 us -> 38.7 us
  waiting for transfers between devices: 54.4 us -> 58.1 us
    ppermute x32, starting transfers between devices: 47 us -> 38.7 us  [ppermute(): return lax.ppermute(value, axis, [(i, target(i)) for i in range(16)])]
    reduce_scatter x1, waiting for transfers between devices: 0.01 us -> 3.42 us  [on_device(): lax.psum_scatter(product, 'tensor', scatter_dimension=0, tiled=True)]
    unnamed x77 -> x81, local copies, waits for them, and re-layouts: 18.2 us -> 18.2 us
  transfers between devices with their start and end apart: 33 -> 33, of which waited for: 11 -> 11; matrix products, arithmetic and copies ran while one was open for 3% -> 6% of each run, Pallas kernels for 19% -> 20%
where the time goes in v1:
time: 195 us; the launch traced here: 194 us
  waiting for transfers between devices  58.1 us (30%)
  Pallas kernels  43.5 us (22%)
  starting transfers between devices  38.7 us (20%)
  local copies, waits for them, and re-layouts  19 us (10%)
  between operations  14.7 us (8%)
  other arithmetic  13.5 us (7%)
  matrix products  6.98 us (4%)
    ppermute x32, waiting for transfers between devices, ppermute(): return lax.ppermute(value, axis, [(i, target(i)) for i in range(16)])  54.6 us
    ppermute x32, starting transfers between devices, ppermute(): return lax.ppermute(value, axis, [(i, target(i)) for i in range(16)])  38.7 us
    unnamed x81, local copies, waits for them, and re-layouts  18.2 us
    pallas_call x2, Pallas kernels, weight_terms(): pl.pallas_call(weight_kernel, grid_spec=pltpu.PrefetchScalarGridSpec(num_...  17.8 us
    pallas_call x5, Pallas kernels, forward(): pl.pallas_call(forward_kernel, grid_spec=pltpu.PrefetchScalarGridSpec(num...  16.5 us
    pallas_call x1, Pallas kernels, scale_sum(): pl.pallas_call(scale_kernel, grid_spec=pltpu.PrefetchScalarGridSpec(num_s...  7.34 us
    dot_general x1, matrix products, backward(): lax.dot_general(dpre, w_in, (((1,), (1,)), ((), ())), preferred_element_t...  6.98 us
  transfers between devices with their start and end apart: 33, of which 11 were waited for; matrix products, arithmetic and copies ran while one was open for 6% of the time, Pallas kernels for 20%

profile of v1, /device:TPU:4, one launch (start us, length us, event | category | flops | bytes accessed | tf_op | source)
XLA Modules:
  0.0 194.5 jit_solution(4344284294075891359)
XLA Ops:
  7.2 1.2 convert_reduce_fusion
  8.4 1.3 fusion.17
  9.7 1.2 fusion.11.refs_0_
  10.9 2.0 %collective-permute-start.1 = (bf16[32,6144]{1,0:T(8,128)(2,1)S(1)}, bf16[32,6144]{1,0:T(8,128)(2,1)}, u32[]{:S(2)}, u32[]{:S(2)}) collective-permute-start(bf16[32,6144]{1,0:T(8,128)(2,1)S(1)} %fusion.11.refs_0_), channel_id=1, source_target_pairs={{0,1},{1,2},{2,3},{3,4},{4,5},{5,6},{6,7},{7,0},{8,9},{9,10},{10,1... | collective-permute-start | bytes 1179656 | tf_op jit(solution)/shard_map/gather/ppermute | solution.py:16
  12.9 4.0 %collective-permute-start = (bf16[32,6144]{1,0:T(8,128)(2,1)S(1)}, bf16[32,6144]{1,0:T(8,128)(2,1)S(1)}, u32[]{:S(2)}, u32[]{:S(2)}) collective-permute-start(bf16[32,6144]{1,0:T(8,128)(2,1)S(1)} %fusion.11.refs_0_), channel_id=1, source_target_pairs={{0,7},{1,0},{2,1},{3,2},{4,3},{5,4},{6,5},{7,6},{8,15},{9,8},{10,9... | collective-permute-start | bytes 1179656 | tf_op jit(solution)/shard_map/gather/ppermute | solution.py:16
  17.0 1.6 collective-permute-start.4
  18.5 7.6 %collective-permute-done.1.refs_2_ = bf16[32,6144]{1,0:T(8,128)(2,1)} collective-permute-done((bf16[32,6144]{1,0:T(8,128)(2,1)S(1)}, bf16[32,6144]{1,0:T(8,128)(2,1)}, u32[]{:S(2)}, u32[]{:S(2)}) %collective-permute-start.1) | collective-permute-done | bytes 393248 | tf_op jit(solution)/shard_map/gather/ppermute | solution.py:16
  26.1 3.2 %collective-permute-start.2 = (bf16[32,6144]{1,0:T(8,128)(2,1)S(1)}, bf16[32,6144]{1,0:T(8,128)(2,1)S(1)}, u32[]{:S(2)}, u32[]{:S(2)}) collective-permute-start(bf16[32,6144]{1,0:T(8,128)(2,1)S(1)} %collective-permute-done.refs_1_), channel_id=1, source_target_pairs={{0,7},{1,0},{2,1},{3,2},{4,3},{5,4},{6,5},{7,6},{8,15},{9,8},{10,9... | collective-permute-start | bytes 1179656 | tf_op jit(solution)/shard_map/gather/ppermute | solution.py:16
  29.4 1.6 collective-permute-start.9
  31.0 3.7 %copy-done = bf16[6144,768]{1,0:T(8,128)(2,1)S(1)} copy-done((bf16[6144,768]{1,0:T(8,128)(2,1)S(1)}, bf16[6144,768]{1,0:T(8,128)(2,1)}, u32[]{:S(2)}) %copy-start) | copy-done | bytes 9437208
  34.7 4.3 %forward.5.refs_16_.refs_0_ = bf16[128,768]{1,0:T(8,128)(2,1)S(1)} custom-call(s32[4]{0:T(128)S(1)} %pad_add_fusion.slots, bf16[32,6144]{1,0:T(8,128)(2,1)S(1)} %fusion.11.refs_0_, bf16[32,6144]{1,0:T(8,128)(2,1)S(1)} %collective-permute-done.refs_1_, bf16[32,6144]{1,0:T(8,128)(2,1)} %collective-permute-done.1.refs_2_, ...), custom_call_target="tpu_custom_call" | custom-call | flops 1 | bytes 1 | tf_op jit(solution)/shard_map/gather/forward/pallas_call | solution.py:120
  39.0 0.7 copy-done.20
  39.7 1.8 collective-permute-start.5
  41.5 0.3 collective-permute-start.8
  41.8 0.4 collective-permute-start.6
  42.2 0.7 pad_add_fusion.2.place
  43.1 3.7 %copy-done.1 = bf16[6144,768]{1,0:T(8,128)(2,1)S(1)} copy-done((bf16[6144,768]{1,0:T(8,128)(2,1)S(1)}, bf16[6144,768]{1,0:T(8,128)(2,1)}, u32[]{:S(2)}) %copy-start.1) | copy-done | bytes 9437208
  46.8 3.1 %forward.6.refs_17_.refs_1_ = bf16[96,768]{1,0:T(8,128)(2,1)S(1)} custom-call(s32[3]{0:T(128)S(1)} %pad_add_fusion.3.slots, bf16[32,6144]{1,0:T(8,128)(2,1)S(1)} %collective-permute-done.2.refs_0_.refs_4_, bf16[32,6144]{1,0:T(8,128)(2,1)S(1)} %collective-permute-done.3.refs_1_.refs_5_, bf16[32,6144]{1,0:T(8,128)(2,1)S(1)} %collective-permute-done.9.refs_2_.refs_6_, ...), custom_call_target="tpu_custom_call" | custom-call | flops 1 | bytes 1 | tf_op jit(solution)/shard_map/gather/forward/pallas_call | solution.py:120
  49.9 0.7 copy-done.22
  50.5 1.0 collective-permute-done.8.refs_1_.refs_8_
  51.6 2.2 %collective-permute-start.7 = (bf16[32,6144]{1,0:T(8,128)(2,1)S(1)}, bf16[32,6144]{1,0:T(8,128)(2,1)S(1)}, u32[]{:S(2)}, u32[]{:S(2)}) collective-permute-start(bf16[32,6144]{1,0:T(8,128)(2,1)S(1)} %collective-permute-done.6.refs_2_.refs_9_), channel_id=1, source_target_pairs={{0,7},{1,0},{2,1},{3,2},{4,3},{5,4},{6,5},{7,6},{8,15},{9,8},{10,9... | collective-permute-start | bytes 1179656 | tf_op jit(solution)/shard_map/gather/ppermute | solution.py:16
  53.8 1.4 collective-permute-start.11
  55.2 3.7 %copy-done.2 = bf16[6144,768]{1,0:T(8,128)(2,1)S(1)} copy-done((bf16[6144,768]{1,0:T(8,128)(2,1)S(1)}, bf16[6144,768]{1,0:T(8,128)(2,1)}, u32[]{:S(2)}) %copy-start.2) | copy-done | bytes 9437208
  58.9 3.1 %forward.7.refs_18_.refs_2_ = bf16[96,768]{1,0:T(8,128)(2,1)S(1)} custom-call(s32[3]{0:T(128)S(1)} %pad_add_fusion.4.slots, bf16[32,6144]{1,0:T(8,128)(2,1)S(1)} %collective-permute-done.5.refs_0_.refs_7_, bf16[32,6144]{1,0:T(8,128)(2,1)S(1)} %collective-permute-done.8.refs_1_.refs_8_, bf16[32,6144]{1,0:T(8,128)(2,1)S(1)} %collective-permute-done.6.refs_2_.refs_9_, ...), custom_call_target="tpu_custom_call" | custom-call | flops 1 | bytes 1 | tf_op jit(solution)/shard_map/gather/forward/pallas_call | solution.py:120
  62.0 0.7 copy-done.24
  62.7 0.3 collective-permute-done.10.refs_1_.refs_11_
  63.1 3.2 %collective-permute-start.12 = (bf16[32,6144]{1,0:T(8,128)(2,1)S(1)}, bf16[32,6144]{1,0:T(8,128)(2,1)S(1)}, u32[]{:S(2)}, u32[]{:S(2)}) collective-permute-start(bf16[32,6144]{1,0:T(8,128)(2,1)S(1)} %collective-permute-done.7.refs_0_.refs_10_), channel_id=1, source_target_pairs={{0,7},{1,0},{2,1},{3,2},{4,3},{5,4},{6,5},{7,6},{8,15},{9,8},{10,9... | collective-permute-start | bytes 1179656 | tf_op jit(solution)/shard_map/gather/ppermute | solution.py:16
  66.3 1.4 collective-permute-start.14
  68.0 3.7 %copy-done.3 = bf16[6144,768]{1,0:T(8,128)(2,1)S(1)} copy-done((bf16[6144,768]{1,0:T(8,128)(2,1)S(1)}, bf16[6144,768]{1,0:T(8,128)(2,1)}, u32[]{:S(2)}) %copy-start.3) | copy-done | bytes 9437208
  71.6 3.1 %forward.8.refs_19_.refs_3_ = bf16[96,768]{1,0:T(8,128)(2,1)S(1)} custom-call(s32[3]{0:T(128)S(1)} %pad_add_fusion.5.slots, bf16[32,6144]{1,0:T(8,128)(2,1)S(1)} %collective-permute-done.7.refs_0_.refs_10_, bf16[32,6144]{1,0:T(8,128)(2,1)S(1)} %collective-permute-done.10.refs_1_.refs_11_, bf16[32,6144]{1,0:T(8,128)(2,1)S(1)} %collective-permute-done.11.refs_2_.refs_12_, ...), custom_call_target="tpu_custom_call" | custom-call | flops 1 | bytes 1 | tf_op jit(solution)/shard_map/gather/forward/pallas_call | solution.py:120
  74.9 3.1 %forward.9.refs_20_.refs_4_ = bf16[96,768]{1,0:T(8,128)(2,1)S(1)} custom-call(s32[3]{0:T(128)S(1)} %pad_add_fusion.6.slots, bf16[32,6144]{1,0:T(8,128)(2,1)S(1)} %collective-permute-done.12.refs_0_.refs_13_, bf16[32,6144]{1,0:T(8,128)(2,1)S(1)} %collective-permute-done.13.refs_1_.refs_14_, bf16[32,6144]{1,0:T(8,128)(2,1)S(1)} %collective-permute-done.14.refs_2_.refs_15_, ...), custom_call_target="tpu_custom_call" | custom-call | flops 1 | bytes 1 | tf_op jit(solution)/shard_map/turn/forward/pallas_call | solution.py:120
  78.0 1.8 place_rows.1
  79.9 7.0 %convolution_convert_fusion.refs_16_ = bf16[512,6144]{1,0:T(8,128)(2,1)} fusion(bf16[512,768]{1,0:T(8,128)(2,1)S(1)} %place_rows.1, bf16[6144,768]{1,0:T(8,128)(2,1)S(1)} %bitcast.65), kind=kOutput, calls=%fused_computation | convolution fusion | flops 4834983936 | bytes 16515072 | tf_op jit(solution)/shard_map/turn/dot_general | solution.py:139
  86.9 0.6 slice.86.order
  87.5 7.3 %scale_sum.1 = f32[8,6144]{1,0:T(8,128)} custom-call(s32[16]{0:T(128)} %copy-done.28, bf16[32,6144]{1,0:T(8,128)(2,1)} %copy-done.5, bf16[32,6144]{1,0:T(8,128)(2,1)} %copy-done.18, bf16[32,6144]{1,0:T(8,128)(2,1)} %collective-permute-done.1.refs_2_, bf16[32,6144]{1,0:T(8,128)(2,1)} %copy-done.19, bf16[32,6144]{1,0:T(8,128)(2,1)} %copy-done.7, ...), custom_call_target="tpu_custom_call" | custom-call | flops 1 | bytes 1 | tf_op jit(solution)/shard_map/weights/scale_sum/pallas_call | solution.py:242
  94.8 1.0 reduce_sum.47
  95.8 6.7 %weight_terms.2 = (bf16[2,768,384]{2,1,0:T(8,128)(2,1)}, bf16[2,768,384]{2,1,0:T(8,128)(2,1)}) custom-call(s32[1]{0:T(128)} %bitcast.68, s32[2]{0:T(128)} %pad_add_fusion.2.place, bf16[32,6144]{1,0:T(8,128)(2,1)} %copy-done.5, bf16[32,6144]{1,0:T(8,128)(2,1)} %copy-done.18, bf16[32,6144]{1,0:T(8,128)(2,1)} %collective-permute-done.1.refs_2_, ...), custom_call_target="tpu_custom_call" | custom-call | flops 4831838208 | bytes 3932160 | tf_op jit(solution)/shard_map/weights/weight_terms/pallas_call | solution.py:175
  102.6 1.2 collective-permute-done.15
  103.8 1.3 collective-permute-start.16
  105.1 11.1 %weight_terms.3 = (bf16[6,768,384]{2,1,0:T(8,128)(2,1)}, bf16[6,768,384]{2,1,0:T(8,128)(2,1)}) custom-call(s32[3]{0:T(128)} %slice.86.order, s32[2]{0:T(128)} %pad_add_fusion.2.place, bf16[32,6144]{1,0:T(8,128)(2,1)} %copy-done.5, bf16[32,6144]{1,0:T(8,128)(2,1)} %copy-done.18, bf16[32,6144]{1,0:T(8,128)(2,1)} %collective-permute-done.1.refs_2_, ...), custom_call_target="tpu_custom_call" | custom-call | flops 14495514624 | bytes 11796480 | tf_op jit(solution)/shard_map/weights/weight_terms/pallas_call | solution.py:175
  116.3 2.8 %collective-permute-done.17 = bf16[2,768,384]{2,1,0:T(8,128)(2,1)S(1)} collective-permute-done((bf16[2,768,384]{2,1,0:T(8,128)(2,1)S(1)}, bf16[2,768,384]{2,1,0:T(8,128)(2,1)S(1)}, u32[]{:S(2)}, u32[]{:S(2)}) %collective-permute-start.17) | collective-permute-done | bytes 1179680 | tf_op jit(solution)/shard_map/core_far/ppermute | solution.py:16
  119.2 0.3 add_convert_fusion
  119.5 0.2 collective-permute-start.20
  119.9 2.0 %collective-permute-start.18 = (bf16[2,384,384]{2,1,0:T(8,128)(2,1)S(1)}, bf16[2,384,384]{2,1,0:T(8,128)(2,1)S(1)}, u32[]{:S(2)}, u32[]{:S(2)}) collective-permute-start(bf16[2,384,384]{2,1,0:T(8,128)(2,1)S(1)} %get-tuple-element.128), channel_id=1, source_target_pairs={{0,64},{16,80},{32,96},{48,112},{64,128},{80,144},{96,160},{112,17... | collective-permute-start | bytes 1769480 | tf_op jit(solution)/shard_map/x_far/ppermute | solution.py:16
  122.0 2.9 %collective-permute-start.21 = (f32[48,128]{1,0:T(8,128)S(1)}, f32[48,128]{1,0:T(8,128)S(1)}, u32[]{:S(2)}, u32[]{:S(2)}) collective-permute-start(f32[48,128]{1,0:T(8,128)S(1)} %add.350), channel_id=1, source_target_pairs={{0,32},{16,48},{32,0},{48,16},{64,96},{80,112},{96,64},{112,80},{1... | collective-permute-start | bytes 73736 | tf_op jit(solution)/shard_map/x_far/ppermute | solution.py:16
  124.9 17.9 %collective-permute-done.21 = f32[48,128]{1,0:T(8,128)S(1)} collective-permute-done((f32[48,128]{1,0:T(8,128)S(1)}, f32[48,128]{1,0:T(8,128)S(1)}, u32[]{:S(2)}, u32[]{:S(2)}) %collective-permute-start.21) | collective-permute-done | bytes 24608 | tf_op jit(solution)/shard_map/x_far/ppermute | solution.py:16
  142.9 0.7 fusion.26
  143.6 0.1 pad_maximum_fusion
  143.8 2.0 %collective-permute-start.23 = (bf16[768,384]{1,0:T(8,128)(2,1)S(1)}, bf16[768,384]{1,0:T(8,128)(2,1)S(1)}, u32[]{:S(2)}, u32[]{:S(2)}) collective-permute-start(bf16[768,384]{1,0:T(8,128)(2,1)S(1)} %get-tuple-element.100), channel_id=1, source_target_pairs={{0,192},{16,208},{32,224},{48,240},{64,0},{80,16},{96,32},{112,48}... | collective-permute-start | bytes 1769480 | tf_op jit(solution)/shard_map/x_other/ppermute | solution.py:16
  145.9 4.1 %collective-permute-done.24 = f32[48,128]{1,0:T(8,128)S(1)} collective-permute-done((f32[48,128]{1,0:T(8,128)S(1)}, f32[48,128]{1,0:T(8,128)S(1)}, u32[]{:S(2)}, u32[]{:S(2)}) %collective-permute-start.24) | collective-permute-done | bytes 24608 | tf_op jit(solution)/shard_map/x_other/ppermute | solution.py:16
  150.0 5.8 %collective-permute-done.25 = f32[48,128]{1,0:T(8,128)S(1)} collective-permute-done((f32[48,128]{1,0:T(8,128)S(1)}, f32[48,128]{1,0:T(8,128)S(1)}, u32[]{:S(2)}, u32[]{:S(2)}) %collective-permute-start.25) | collective-permute-done | bytes 24608 | tf_op jit(solution)/shard_map/x_other/ppermute | solution.py:16
  155.8 0.1 pad_maximum_fusion.2
  155.9 8.3 %collective-permute-done.26 = f32[48,128]{1,0:T(8,128)S(1)} collective-permute-done((f32[48,128]{1,0:T(8,128)S(1)}, f32[48,128]{1,0:T(8,128)S(1)}, u32[]{:S(2)}, u32[]{:S(2)}) %collective-permute-start.26) | collective-permute-done | bytes 24608 | tf_op jit(solution)/shard_map/x_other/ppermute | solution.py:16
  164.3 0.3 fusion.5
  164.7 2.3 %collective-permute-start.28 = (bf16[768,384]{1,0:T(8,128)(2,1)S(1)}, bf16[768,384]{1,0:T(8,128)(2,1)S(1)}, u32[]{:S(2)}, u32[]{:S(2)}) collective-permute-start(bf16[768,384]{1,0:T(8,128)(2,1)S(1)} %get-tuple-element.109), channel_id=1, source_target_pairs={{0,64},{16,80},{32,96},{48,112},{64,128},{80,144},{96,160},{112,17... | collective-permute-start | bytes 1769480 | tf_op jit(solution)/shard_map/x_own/ppermute | solution.py:16
  167.0 3.4 %collective-permute-start.30 = (bf16[768,384]{1,0:T(8,128)(2,1)S(1)}, bf16[768,384]{1,0:T(8,128)(2,1)}, u32[]{:S(2)}, u32[]{:S(2)}) collective-permute-start(bf16[768,384]{1,0:T(8,128)(2,1)S(1)} %fusion.5), channel_id=1, source_target_pairs={{0,32},{16,48},{32,0},{48,16},{64,96},{80,112},{96,64},{112,80},{1... | collective-permute-start | bytes 1769480 | tf_op jit(solution)/shard_map/x_own/ppermute | solution.py:16
  170.4 3.4 %reduce-scatter.2.cloned.1.call-done = bf16[32,6144]{1,0:T(8,128)(2,1)} async-done(((bf16[512,6144]{1,0:T(8,128)(2,1)}), bf16[32,6144]{1,0:T(8,128)(2,1)}) %reduce-scatter.2.cloned.1.call-update) | async-done | bytes 393232 | tf_op jit(solution)/shard_map/scatter/reduce_scatter | solution.py:314
  173.8 1.3 fusion.18
  175.1 2.1 %fusion.16 = bf16[32,6144]{1,0:T(8,128)(2,1)} fusion(bf16[32,6144]{1,0:T(8,128)(2,1)S(1)} %copy-done.29, bf16[32,6144]{1,0:T(8,128)(2,1)} %reduce-scatter.2.cloned.1.call-done, bf16[32,6144]{1,0:T(8,128)(2,1)S(1)} %copy-done.34, f32[32]{0:T(128)S(1)} %get-tuple-element.133, f32[32]{0:T(128)S(1)} %get-tuple-element.134, f32[6144]{0:T(1024)S(1)} %copy-done.33, ...), kind=kLoop, calls=%fused_computation.22 | loop fusion | flops 2359296 | bytes 1597952 | tf_op jit(solution)/shard_map/input_gradient/convert_element_type | solution.py:375
  177.2 0.8 collective-permute-start.31
  178.1 5.6 %collective-permute-done.30 = bf16[768,384]{1,0:T(8,128)(2,1)} collective-permute-done((bf16[768,384]{1,0:T(8,128)(2,1)S(1)}, bf16[768,384]{1,0:T(8,128)(2,1)}, u32[]{:S(2)}, u32[]{:S(2)}) %collective-permute-start.30) | collective-permute-done | bytes 589856 | tf_op jit(solution)/shard_map/x_own/ppermute | solution.py:16
  183.6 2.0 %fusion.3 = f32[384,768]{0,1:T(8,128)S(1)} fusion(bf16[768,384]{1,0:T(8,128)(2,1)} %collective-permute-done.30, bf16[768,384]{1,0:T(8,128)(2,1)} %collective-permute-done.29, bf16[768,384]{1,0:T(8,128)(2,1)S(1)} %collective-permute-done.28, bf16[6,768,384]{2,1,0:T(8,128)(2,1)} %copy-done.31, bf16[6,768,384]{2,1,0:T(8,128)(2,1)} %get-tuple-element.87), kind=kLoop, calls=%fused_computation.6 | loop fusion | flops 2949120 | bytes 4128768 | tf_op jit(solution)/shard_map/x_own/transpose | solution.py:364
  185.6 1.4 copy.8
  187.0 0.6 fusion.27
  (129 shorter events, 1.6 us)
Async XLA Ops:
  7.2 23.9 %copy-start.4 = (bf16[512,768]{1,0:T(8,128)(2,1)S(1)}, bf16[512,768]{1,0:T(8,128)(2,1)}, u32[]{:S(2)}) copy-start(bf16[512,768]{1,0:T(8,128)(2,1)} %refs_6_.9) | copy-start | bytes 2359300
  7.2 166.6 %reduce-scatter.2.cloned.1.call-start = ((), (), s32[]{:S(2)}) async-start(), calls=%async_computation.1 | async-start | bytes 6684672 | tf_op jit(solution)/shard_map/scatter/reduce_scatter | solution.py:314
  10.9 28.0 %copy-start.5 = (bf16[32,6144]{1,0:T(8,128)(2,1)}, bf16[32,6144]{1,0:T(8,128)(2,1)S(1)}, u32[]{:S(2)}) copy-start(bf16[32,6144]{1,0:T(8,128)(2,1)S(1)} %fusion.11.refs_0_) | copy-start | bytes 1179652
  10.9 15.2 %collective-permute-start.1 = (bf16[32,6144]{1,0:T(8,128)(2,1)S(1)}, bf16[32,6144]{1,0:T(8,128)(2,1)}, u32[]{:S(2)}, u32[]{:S(2)}) collective-permute-start(bf16[32,6144]{1,0:T(8,128)(2,1)S(1)} %fusion.11.refs_0_), channel_id=1, source_target_pairs={{0,1},{1,2},{2,3},{3,4},{4,5},{5,6},{6,7},{7,0},{8,9},{9,10},{10,1... | collective-permute-start | bytes 1179656 | tf_op jit(solution)/shard_map/gather/ppermute | solution.py:16
  12.9 13.2 %collective-permute-start = (bf16[32,6144]{1,0:T(8,128)(2,1)S(1)}, bf16[32,6144]{1,0:T(8,128)(2,1)S(1)}, u32[]{:S(2)}, u32[]{:S(2)}) collective-permute-start(bf16[32,6144]{1,0:T(8,128)(2,1)S(1)} %fusion.11.refs_0_), channel_id=1, source_target_pairs={{0,7},{1,0},{2,1},{3,2},{4,3},{5,4},{6,5},{7,6},{8,15},{9,8},{10,9... | collective-permute-start | bytes 1179656 | tf_op jit(solution)/shard_map/gather/ppermute | solution.py:16
  17.0 14.1 %collective-permute-start.4 = (bf16[32,6144]{1,0:T(8,128)(2,1)S(1)}, bf16[32,6144]{1,0:T(8,128)(2,1)S(1)}, u32[]{:S(2)}, u32[]{:S(2)}) collective-permute-start(bf16[32,6144]{1,0:T(8,128)(2,1)S(1)} %fusion.11.refs_0_), channel_id=1, source_target_pairs={{0,8},{1,9},{2,10},{3,11},{4,12},{5,13},{6,14},{7,15},{8,0},{9,1},... | collective-permute-start | bytes 1179656 | tf_op jit(solution)/shard_map/gather/ppermute | solution.py:16
  26.1 12.9 %copy-start.18 = (bf16[32,6144]{1,0:T(8,128)(2,1)}, bf16[32,6144]{1,0:T(8,128)(2,1)S(1)}, u32[]{:S(2)}) copy-start(bf16[32,6144]{1,0:T(8,128)(2,1)S(1)} %collective-permute-done.refs_1_) | copy-start | bytes 1179652
  26.1 13.6 %collective-permute-start.3 = (bf16[32,6144]{1,0:T(8,128)(2,1)}, bf16[32,6144]{1,0:T(8,128)(2,1)S(1)}, u32[]{:S(2)}, u32[]{:S(2)}) collective-permute-start(bf16[32,6144]{1,0:T(8,128)(2,1)} %collective-permute-done.1.refs_2_), channel_id=1, source_target_pairs={{0,1},{1,2},{2,3},{3,4},{4,5},{5,6},{6,7},{7,0},{8,9},{9,10},{10,1... | collective-permute-start | bytes 1179656 | tf_op jit(solution)/shard_map/gather/ppermute | solution.py:16
  26.1 13.6 %collective-permute-start.2 = (bf16[32,6144]{1,0:T(8,128)(2,1)S(1)}, bf16[32,6144]{1,0:T(8,128)(2,1)S(1)}, u32[]{:S(2)}, u32[]{:S(2)}) collective-permute-start(bf16[32,6144]{1,0:T(8,128)(2,1)S(1)} %collective-permute-done.refs_1_), channel_id=1, source_target_pairs={{0,7},{1,0},{2,1},{3,2},{4,3},{5,4},{6,5},{7,6},{8,15},{9,8},{10,9... | collective-permute-start | bytes 1179656 | tf_op jit(solution)/shard_map/gather/ppermute | solution.py:16
  29.4 13.7 %collective-permute-start.9 = (bf16[32,6144]{1,0:T(8,128)(2,1)S(1)}, bf16[32,6144]{1,0:T(8,128)(2,1)S(1)}, u32[]{:S(2)}, u32[]{:S(2)}) collective-permute-start(bf16[32,6144]{1,0:T(8,128)(2,1)S(1)} %collective-permute-done.refs_1_), channel_id=1, source_target_pairs={{0,8},{1,9},{2,10},{3,11},{4,12},{5,13},{6,14},{7,15},{8,0},{9,1},... | collective-permute-start | bytes 1179656 | tf_op jit(solution)/shard_map/gather/ppermute | solution.py:16
  31.0 3.7 %copy-start = (bf16[6144,768]{1,0:T(8,128)(2,1)S(1)}, bf16[6144,768]{1,0:T(8,128)(2,1)}, u32[]{:S(2)}) copy-start(bf16[6144,768]{1,0:T(8,128)(2,1)} %refs_3_.7) | copy-start | bytes 28311556
  34.7 4.3 %copy-start.19 = (bf16[32,6144]{1,0:T(8,128)(2,1)}, bf16[32,6144]{1,0:T(8,128)(2,1)S(1)}, u32[]{:S(2)}) copy-start(bf16[32,6144]{1,0:T(8,128)(2,1)S(1)} %collective-permute-done.4.refs_3_) | copy-start | bytes 1179652
  39.7 14.1 %copy-start.6 = (bf16[32,6144]{1,0:T(8,128)(2,1)}, bf16[32,6144]{1,0:T(8,128)(2,1)S(1)}, u32[]{:S(2)}) copy-start(bf16[32,6144]{1,0:T(8,128)(2,1)S(1)} %collective-permute-done.3.refs_1_.refs_5_) | copy-start | bytes 1179652
  39.7 10.1 %copy-start.7 = (bf16[32,6144]{1,0:T(8,128)(2,1)}, bf16[32,6144]{1,0:T(8,128)(2,1)S(1)}, u32[]{:S(2)}) copy-start(bf16[32,6144]{1,0:T(8,128)(2,1)S(1)} %collective-permute-done.2.refs_0_.refs_4_) | copy-start | bytes 1179652
  39.7 10.8 %collective-permute-start.5 = (bf16[32,6144]{1,0:T(8,128)(2,1)S(1)}, bf16[32,6144]{1,0:T(8,128)(2,1)S(1)}, u32[]{:S(2)}, u32[]{:S(2)}) collective-permute-start(bf16[32,6144]{1,0:T(8,128)(2,1)S(1)} %collective-permute-done.2.refs_0_.refs_4_), channel_id=1, source_target_pairs={{0,7},{1,0},{2,1},{3,2},{4,3},{5,4},{6,5},{7,6},{8,15},{9,8},{10,9... | collective-permute-start | bytes 1179656 | tf_op jit(solution)/shard_map/gather/ppermute | solution.py:16
  41.5 10.1 %collective-permute-start.8 = (bf16[32,6144]{1,0:T(8,128)(2,1)S(1)}, bf16[32,6144]{1,0:T(8,128)(2,1)S(1)}, u32[]{:S(2)}, u32[]{:S(2)}) collective-permute-start(bf16[32,6144]{1,0:T(8,128)(2,1)S(1)} %collective-permute-done.3.refs_1_.refs_5_), channel_id=1, source_target_pairs={{0,1},{1,2},{2,3},{3,4},{4,5},{5,6},{6,7},{7,0},{8,9},{9,10},{10,1... | collective-permute-start | bytes 1179656 | tf_op jit(solution)/shard_map/gather/ppermute | solution.py:16
  41.8 9.8 %collective-permute-start.6 = (bf16[32,6144]{1,0:T(8,128)(2,1)S(1)}, bf16[32,6144]{1,0:T(8,128)(2,1)S(1)}, u32[]{:S(2)}, u32[]{:S(2)}) collective-permute-start(bf16[32,6144]{1,0:T(8,128)(2,1)S(1)} %collective-permute-done.2.refs_0_.refs_4_), channel_id=1, source_target_pairs={{0,8},{1,9},{2,10},{3,11},{4,12},{5,13},{6,14},{7,15},{8,0},{9,1},... | collective-permute-start | bytes 1179656 | tf_op jit(solution)/shard_map/gather/ppermute | solution.py:16
  43.1 43.8 %copy-start.35 = (s32[4]{0:T(128)}, s32[4]{0:T(128)S(1)}, u32[]{:S(2)}) copy-start(s32[4]{0:T(128)S(1)} %pad_add_fusion.1) | copy-start | bytes 52
  43.1 3.7 %copy-start.1 = (bf16[6144,768]{1,0:T(8,128)(2,1)S(1)}, bf16[6144,768]{1,0:T(8,128)(2,1)}, u32[]{:S(2)}) copy-start(bf16[6144,768]{1,0:T(8,128)(2,1)} %refs_3_.7) | copy-start | bytes 28311556
  50.5 11.5 %copy-start.9 = (bf16[32,6144]{1,0:T(8,128)(2,1)}, bf16[32,6144]{1,0:T(8,128)(2,1)S(1)}, u32[]{:S(2)}) copy-start(bf16[32,6144]{1,0:T(8,128)(2,1)S(1)} %collective-permute-done.5.refs_0_.refs_7_) | copy-start | bytes 1179652
  51.6 10.4 %copy-start.10 = (bf16[32,6144]{1,0:T(8,128)(2,1)}, bf16[32,6144]{1,0:T(8,128)(2,1)S(1)}, u32[]{:S(2)}) copy-start(bf16[32,6144]{1,0:T(8,128)(2,1)S(1)} %collective-permute-done.8.refs_1_.refs_8_) | copy-start | bytes 1179652
  51.6 10.4 %copy-start.11 = (bf16[32,6144]{1,0:T(8,128)(2,1)}, bf16[32,6144]{1,0:T(8,128)(2,1)S(1)}, u32[]{:S(2)}) copy-start(bf16[32,6144]{1,0:T(8,128)(2,1)S(1)} %collective-permute-done.6.refs_2_.refs_9_) | copy-start | bytes 1179652
  51.6 11.1 %collective-permute-start.7 = (bf16[32,6144]{1,0:T(8,128)(2,1)S(1)}, bf16[32,6144]{1,0:T(8,128)(2,1)S(1)}, u32[]{:S(2)}, u32[]{:S(2)}) collective-permute-start(bf16[32,6144]{1,0:T(8,128)(2,1)S(1)} %collective-permute-done.6.refs_2_.refs_9_), channel_id=1, source_target_pairs={{0,7},{1,0},{2,1},{3,2},{4,3},{5,4},{6,5},{7,6},{8,15},{9,8},{10,9... | collective-permute-start | bytes 1179656 | tf_op jit(solution)/shard_map/gather/ppermute | solution.py:16
  53.8 9.2 %collective-permute-start.10 = (bf16[32,6144]{1,0:T(8,128)(2,1)S(1)}, bf16[32,6144]{1,0:T(8,128)(2,1)S(1)}, u32[]{:S(2)}, u32[]{:S(2)}) collective-permute-start(bf16[32,6144]{1,0:T(8,128)(2,1)S(1)} %collective-permute-done.8.refs_1_.refs_8_), channel_id=1, source_target_pairs={{0,1},{1,2},{2,3},{3,4},{4,5},{5,6},{6,7},{7,0},{8,9},{9,10},{10,1... | collective-permute-start | bytes 1179656 | tf_op jit(solution)/shard_map/gather/ppermute | solution.py:16
  53.8 9.2 %collective-permute-start.11 = (bf16[32,6144]{1,0:T(8,128)(2,1)S(1)}, bf16[32,6144]{1,0:T(8,128)(2,1)S(1)}, u32[]{:S(2)}, u32[]{:S(2)}) collective-permute-start(bf16[32,6144]{1,0:T(8,128)(2,1)S(1)} %collective-permute-done.3.refs_1_.refs_5_), channel_id=1, source_target_pairs={{0,8},{1,9},{2,10},{3,11},{4,12},{5,13},{6,14},{7,15},{8,0},{9,1},... | collective-permute-start | bytes 1179656 | tf_op jit(solution)/shard_map/gather/ppermute | solution.py:16
  55.2 3.7 %copy-start.2 = (bf16[6144,768]{1,0:T(8,128)(2,1)S(1)}, bf16[6144,768]{1,0:T(8,128)(2,1)}, u32[]{:S(2)}) copy-start(bf16[6144,768]{1,0:T(8,128)(2,1)} %refs_3_.7) | copy-start | bytes 28311556
  62.7 12.0 %copy-start.12 = (bf16[32,6144]{1,0:T(8,128)(2,1)}, bf16[32,6144]{1,0:T(8,128)(2,1)S(1)}, u32[]{:S(2)}) copy-start(bf16[32,6144]{1,0:T(8,128)(2,1)S(1)} %collective-permute-done.7.refs_0_.refs_10_) | copy-start | bytes 1179652
  63.0 11.8 %copy-start.13 = (bf16[32,6144]{1,0:T(8,128)(2,1)}, bf16[32,6144]{1,0:T(8,128)(2,1)S(1)}, u32[]{:S(2)}) copy-start(bf16[32,6144]{1,0:T(8,128)(2,1)S(1)} %collective-permute-done.10.refs_1_.refs_11_) | copy-start | bytes 1179652
  63.0 11.8 %copy-start.14 = (bf16[32,6144]{1,0:T(8,128)(2,1)}, bf16[32,6144]{1,0:T(8,128)(2,1)S(1)}, u32[]{:S(2)}) copy-start(bf16[32,6144]{1,0:T(8,128)(2,1)S(1)} %collective-permute-done.11.refs_2_.refs_12_) | copy-start | bytes 1179652
  63.0 11.8 %collective-permute-start.13 = (bf16[32,6144]{1,0:T(8,128)(2,1)S(1)}, bf16[32,6144]{1,0:T(8,128)(2,1)S(1)}, u32[]{:S(2)}, u32[]{:S(2)}) collective-permute-start(bf16[32,6144]{1,0:T(8,128)(2,1)S(1)} %collective-permute-done.11.refs_2_.refs_12_), channel_id=1, source_target_pairs={{0,1},{1,2},{2,3},{3,4},{4,5},{5,6},{6,7},{7,0},{8,9},{9,10},{10,1... | collective-permute-start | bytes 1179656 | tf_op jit(solution)/shard_map/gather/ppermute | solution.py:16
  63.1 11.8 %collective-permute-start.12 = (bf16[32,6144]{1,0:T(8,128)(2,1)S(1)}, bf16[32,6144]{1,0:T(8,128)(2,1)S(1)}, u32[]{:S(2)}, u32[]{:S(2)}) collective-permute-start(bf16[32,6144]{1,0:T(8,128)(2,1)S(1)} %collective-permute-done.7.refs_0_.refs_10_), channel_id=1, source_target_pairs={{0,7},{1,0},{2,1},{3,2},{4,3},{5,4},{6,5},{7,6},{8,15},{9,8},{10,9... | collective-permute-start | bytes 1179656 | tf_op jit(solution)/shard_map/gather/ppermute | solution.py:16
  66.3 8.5 %collective-permute-start.14 = (bf16[32,6144]{1,0:T(8,128)(2,1)}, bf16[32,6144]{1,0:T(8,128)(2,1)S(1)}, u32[]{:S(2)}, u32[]{:S(2)}) collective-permute-start(bf16[32,6144]{1,0:T(8,128)(2,1)} %collective-permute-done.1.refs_2_), channel_id=1, source_target_pairs={{0,8},{1,9},{2,10},{3,11},{4,12},{5,13},{6,14},{7,15},{8,0},{9,1},... | collective-permute-start | bytes 1179656 | tf_op jit(solution)/shard_map/gather/ppermute | solution.py:16
  67.8 10.2 %copy-start.28 = (s32[16]{0:T(128)}, s32[16]{0:T(128)S(1)}, u32[]{:S(2)}) copy-start(s32[16]{0:T(128)S(1)} %stack.135.slots) | copy-start | bytes 196
  68.0 3.7 %copy-start.3 = (bf16[6144,768]{1,0:T(8,128)(2,1)S(1)}, bf16[6144,768]{1,0:T(8,128)(2,1)}, u32[]{:S(2)}) copy-start(bf16[6144,768]{1,0:T(8,128)(2,1)} %refs_3_.7) | copy-start | bytes 28311556
  71.6 8.2 %slice-start = ((s8[9437184]{0:T(1024)(128)(4,1)}), s8[4194304]{0:T(1024)(128)(4,1)S(1)}, s32[]{:S(2)}) async-start(s8[9437184]{0:T(1024)(128)(4,1)} %bitcast.64), calls=%async_computation.2 | async-start | bytes 8388608
  71.6 8.2 %slice-start.1 = ((s8[9437184]{0:T(1024)(128)(4,1)}), s8[4194304]{0:T(1024)(128)(4,1)S(1)}, s32[]{:S(2)}) async-start(s8[9437184]{0:T(1024)(128)(4,1)} %bitcast.64), calls=%async_computation.3 | async-start | bytes 8388608
  74.8 3.2 %copy-start.21 = (bf16[128,768]{1,0:T(8,128)(2,1)S(1)}, bf16[128,768]{1,0:T(8,128)(2,1)}, u32[]{:S(2)}) copy-start(bf16[128,768]{1,0:T(8,128)(2,1)} %copy-done.20) | copy-start | bytes 589828
  74.8 3.2 %copy-start.23 = (bf16[96,768]{1,0:T(8,128)(2,1)S(1)}, bf16[96,768]{1,0:T(8,128)(2,1)}, u32[]{:S(2)}) copy-start(bf16[96,768]{1,0:T(8,128)(2,1)} %copy-done.22) | copy-start | bytes 442372
  74.8 5.1 %slice-start.2 = ((s8[9437184]{0:T(1024)(128)(4,1)}), s8[1048576]{0:T(1024)(128)(4,1)S(1)}, s32[]{:S(2)}) async-start(s8[9437184]{0:T(1024)(128)(4,1)} %bitcast.64), calls=%async_computation.4 | async-start | bytes 2097152
  78.0 8.8 %copy-start.27 = (bf16[96,768]{1,0:T(8,128)(2,1)}, bf16[96,768]{1,0:T(8,128)(2,1)S(1)}, u32[]{:S(2)}) copy-start(bf16[96,768]{1,0:T(8,128)(2,1)S(1)} %forward.9.refs_20_.refs_4_) | copy-start | bytes 442372
  102.5 1.3 collective-permute-start.15
  103.8 12.4 %copy-start.36 = (bf16[2,768,384]{2,1,0:T(8,128)(2,1)S(1)}, bf16[2,768,384]{2,1,0:T(8,128)(2,1)}, u32[]{:S(2)}) copy-start(bf16[2,768,384]{2,1,0:T(8,128)(2,1)} %get-tuple-element.89) | copy-start | bytes 3538948
  103.8 15.4 %copy-start.32 = (bf16[2,768,384]{2,1,0:T(8,128)(2,1)S(1)}, bf16[2,768,384]{2,1,0:T(8,128)(2,1)}, u32[]{:S(2)}) copy-start(bf16[2,768,384]{2,1,0:T(8,128)(2,1)} %get-tuple-element.88) | copy-start | bytes 3538948
  103.8 12.4 %collective-permute-start.16 = (f32[48,128]{1,0:T(8,128)S(1)}, f32[48,128]{1,0:T(8,128)S(1)}, u32[]{:S(2)}, u32[]{:S(2)}) collective-permute-start(f32[48,128]{1,0:T(8,128)S(1)} %add.349), channel_id=1, source_target_pairs={{0,64},{16,80},{32,96},{48,112},{64,0},{80,16},{96,32},{112,48},{1... | collective-permute-start | bytes 73736 | tf_op jit(solution)/shard_map/weights/ppermute | solution.py:16
  116.2 2.9 %collective-permute-start.17 = (bf16[2,768,384]{2,1,0:T(8,128)(2,1)S(1)}, bf16[2,768,384]{2,1,0:T(8,128)(2,1)S(1)}, u32[]{:S(2)}, u32[]{:S(2)}) collective-permute-start(bf16[2,768,384]{2,1,0:T(8,128)(2,1)S(1)} %copy-done.36), channel_id=1, source_target_pairs={{0,16},{16,0},{32,48},{48,32},{64,80},{80,64},{96,112},{112,96},{1... | collective-permute-start | bytes 3538952 | tf_op jit(solution)/shard_map/core_far/ppermute | solution.py:16
  119.2 23.6 %copy-start.30 = (bf16[6,768,384]{2,1,0:T(8,128)(2,1)S(1)}, bf16[6,768,384]{2,1,0:T(8,128)(2,1)}, u32[]{:S(2)}) copy-start(bf16[6,768,384]{2,1,0:T(8,128)(2,1)} %get-tuple-element.87) | copy-start | bytes 10616836
  119.5 23.3 %collective-permute-start.20 = (bf16[6,768,384]{2,1,0:T(8,128)(2,1)}, bf16[6,768,384]{2,1,0:T(8,128)(2,1)S(1)}, u32[]{:S(2)}, u32[]{:S(2)}) collective-permute-start(bf16[6,768,384]{2,1,0:T(8,128)(2,1)} %get-tuple-element.93), channel_id=1, source_target_pairs={{0,16},{16,0},{32,48},{48,32},{64,80},{80,64},{96,112},{112,96},{1... | collective-permute-start | bytes 10616840 | tf_op jit(solution)/shard_map/x_far/ppermute | solution.py:16
  119.8 22.9 %collective-permute-start.19 = (bf16[2,384,384]{2,1,0:T(8,128)(2,1)S(1)}, bf16[2,384,384]{2,1,0:T(8,128)(2,1)S(1)}, u32[]{:S(2)}, u32[]{:S(2)}) collective-permute-start(bf16[2,384,384]{2,1,0:T(8,128)(2,1)S(1)} %get-tuple-element.127), channel_id=1, source_target_pairs={{0,192},{16,208},{32,224},{48,240},{64,0},{80,16},{96,32},{112,48}... | collective-permute-start | bytes 1769480 | tf_op jit(solution)/shard_map/x_far/ppermute | solution.py:16
  119.9 22.8 %collective-permute-start.18 = (bf16[2,384,384]{2,1,0:T(8,128)(2,1)S(1)}, bf16[2,384,384]{2,1,0:T(8,128)(2,1)S(1)}, u32[]{:S(2)}, u32[]{:S(2)}) collective-permute-start(bf16[2,384,384]{2,1,0:T(8,128)(2,1)S(1)} %get-tuple-element.128), channel_id=1, source_target_pairs={{0,64},{16,80},{32,96},{48,112},{64,128},{80,144},{96,160},{112,17... | collective-permute-start | bytes 1769480 | tf_op jit(solution)/shard_map/x_far/ppermute | solution.py:16
  122.0 20.8 %collective-permute-start.21 = (f32[48,128]{1,0:T(8,128)S(1)}, f32[48,128]{1,0:T(8,128)S(1)}, u32[]{:S(2)}, u32[]{:S(2)}) collective-permute-start(f32[48,128]{1,0:T(8,128)S(1)} %add.350), channel_id=1, source_target_pairs={{0,32},{16,48},{32,0},{48,16},{64,96},{80,112},{96,64},{112,80},{1... | collective-permute-start | bytes 73736 | tf_op jit(solution)/shard_map/x_far/ppermute | solution.py:16
  142.8 21.5 %copy-start.31 = (bf16[6,768,384]{2,1,0:T(8,128)(2,1)}, bf16[6,768,384]{2,1,0:T(8,128)(2,1)S(1)}, u32[]{:S(2)}) copy-start(bf16[6,768,384]{2,1,0:T(8,128)(2,1)S(1)} %collective-permute-done.20) | copy-start | bytes 10616836
  143.8 20.5 %collective-permute-start.22 = (bf16[768,384]{1,0:T(8,128)(2,1)S(1)}, bf16[768,384]{1,0:T(8,128)(2,1)S(1)}, u32[]{:S(2)}, u32[]{:S(2)}) collective-permute-start(bf16[768,384]{1,0:T(8,128)(2,1)S(1)} %get-tuple-element.99), channel_id=1, source_target_pairs={{0,64},{16,80},{32,96},{48,112},{64,128},{80,144},{96,160},{112,17... | collective-permute-start | bytes 1769480 | tf_op jit(solution)/shard_map/x_other/ppermute | solution.py:16
  143.8 20.4 %collective-permute-start.23 = (bf16[768,384]{1,0:T(8,128)(2,1)S(1)}, bf16[768,384]{1,0:T(8,128)(2,1)S(1)}, u32[]{:S(2)}, u32[]{:S(2)}) collective-permute-start(bf16[768,384]{1,0:T(8,128)(2,1)S(1)} %get-tuple-element.100), channel_id=1, source_target_pairs={{0,192},{16,208},{32,224},{48,240},{64,0},{80,16},{96,32},{112,48}... | collective-permute-start | bytes 1769480 | tf_op jit(solution)/shard_map/x_other/ppermute | solution.py:16
  145.9 4.2 %collective-permute-start.24 = (f32[48,128]{1,0:T(8,128)S(1)}, f32[48,128]{1,0:T(8,128)S(1)}, u32[]{:S(2)}, u32[]{:S(2)}) collective-permute-start(f32[48,128]{1,0:T(8,128)S(1)} %add.352), channel_id=1, source_target_pairs={{0,1},{1,0},{2,3},{3,2},{4,5},{5,4},{6,7},{7,6},{8,9},{9,8},{10,11... | collective-permute-start | bytes 73736 | tf_op jit(solution)/shard_map/x_other/ppermute | solution.py:16
  150.0 5.8 %collective-permute-start.25 = (f32[48,128]{1,0:T(8,128)S(1)}, f32[48,128]{1,0:T(8,128)S(1)}, u32[]{:S(2)}, u32[]{:S(2)}) collective-permute-start(f32[48,128]{1,0:T(8,128)S(1)} %add.365), channel_id=1, source_target_pairs={{0,2},{1,3},{2,0},{3,1},{4,6},{5,7},{6,4},{7,5},{8,10},{9,11},{10,... | collective-permute-start | bytes 73736 | tf_op jit(solution)/shard_map/x_other/ppermute | solution.py:16
  155.8 8.4 %collective-permute-start.26 = (f32[48,128]{1,0:T(8,128)S(1)}, f32[48,128]{1,0:T(8,128)S(1)}, u32[]{:S(2)}, u32[]{:S(2)}) collective-permute-start(f32[48,128]{1,0:T(8,128)S(1)} %add.366), channel_id=1, source_target_pairs={{0,4},{1,5},{2,6},{3,7},{4,0},{5,1},{6,2},{7,3},{8,12},{9,13},{10,... | collective-permute-start | bytes 73736 | tf_op jit(solution)/shard_map/x_other/ppermute | solution.py:16
  164.3 9.5 %copy-start.29 = (bf16[32,6144]{1,0:T(8,128)(2,1)S(1)}, bf16[32,6144]{1,0:T(8,128)(2,1)}, u32[]{:S(2)}) copy-start(bf16[32,6144]{1,0:T(8,128)(2,1)} %param.5) | copy-start | bytes 1179652
  164.3 9.5 %copy-start.33 = (f32[6144]{0:T(1024)S(1)}, f32[6144]{0:T(1024)}, u32[]{:S(2)}) copy-start(f32[6144]{0:T(1024)} %param.6) | copy-start | bytes 73732
  164.3 10.8 %copy-start.34 = (bf16[32,6144]{1,0:T(8,128)(2,1)S(1)}, bf16[32,6144]{1,0:T(8,128)(2,1)}, u32[]{:S(2)}) copy-start(bf16[32,6144]{1,0:T(8,128)(2,1)} %param.9) | copy-start | bytes 1179652
  164.6 12.6 %collective-permute-start.27 = (f32[48,128]{1,0:T(8,128)S(1)}, f32[48,128]{1,0:T(8,128)S(1)}, u32[]{:S(2)}, u32[]{:S(2)}) collective-permute-start(f32[48,128]{1,0:T(8,128)S(1)} %add.367), channel_id=1, source_target_pairs={{0,128},{16,144},{32,160},{48,176},{64,192},{80,208},{96,224},{112... | collective-permute-start | bytes 73736 | tf_op jit(solution)/shard_map/x_own/ppermute | solution.py:16
  164.7 13.4 %collective-permute-start.28 = (bf16[768,384]{1,0:T(8,128)(2,1)S(1)}, bf16[768,384]{1,0:T(8,128)(2,1)S(1)}, u32[]{:S(2)}, u32[]{:S(2)}) collective-permute-start(bf16[768,384]{1,0:T(8,128)(2,1)S(1)} %get-tuple-element.109), channel_id=1, source_target_pairs={{0,64},{16,80},{32,96},{48,112},{64,128},{80,144},{96,160},{112,17... | collective-permute-start | bytes 1769480 | tf_op jit(solution)/shard_map/x_own/ppermute | solution.py:16
  167.0 11.1 %collective-permute-start.29 = (bf16[768,384]{1,0:T(8,128)(2,1)S(1)}, bf16[768,384]{1,0:T(8,128)(2,1)}, u32[]{:S(2)}, u32[]{:S(2)}) collective-permute-start(bf16[768,384]{1,0:T(8,128)(2,1)S(1)} %get-tuple-element.110), channel_id=1, source_target_pairs={{0,192},{16,208},{32,224},{48,240},{64,0},{80,16},{96,32},{112,48}... | collective-permute-start | bytes 1769480 | tf_op jit(solution)/shard_map/x_own/ppermute | solution.py:16
  167.0 16.7 %collective-permute-start.30 = (bf16[768,384]{1,0:T(8,128)(2,1)S(1)}, bf16[768,384]{1,0:T(8,128)(2,1)}, u32[]{:S(2)}, u32[]{:S(2)}) collective-permute-start(bf16[768,384]{1,0:T(8,128)(2,1)S(1)} %fusion.5), channel_id=1, source_target_pairs={{0,32},{16,48},{32,0},{48,16},{64,96},{80,112},{96,64},{112,80},{1... | collective-permute-start | bytes 1769480 | tf_op jit(solution)/shard_map/x_own/ppermute | solution.py:16
  177.2 9.8 %collective-permute-start.31 = (f32[48,128]{1,0:T(8,128)S(1)}, f32[48,128]{1,0:T(8,128)S(1)}, u32[]{:S(2)}, u32[]{:S(2)}) collective-permute-start(f32[48,128]{1,0:T(8,128)S(1)} %add.378), channel_id=1, source_target_pairs={{0,8},{1,9},{2,10},{3,11},{4,12},{5,13},{6,14},{7,15},{8,0},{9,1},... | collective-permute-start | bytes 73736 | tf_op jit(solution)/shard_map/scale_gradient/ppermute | solution.py:16
  (9 other events, 21.0 us)
Sparse Core Ops, SparseCore 0:
  87.0 86.7 reduce-scatter.1

commit v2 on v1

--- a/solution.py
+++ b/solution.py
@@ -362,6 +362,7 @@
         for value in (up_moved, down_moved, from_y):
             own = own + value.astype(F32)
         grad_w = (own / 16).T
+        total = together(total, normed_gradient[:1, :1])[0]
         last = ppermute(total, "dp", lambda i: i ^ 8)
 
     with jax.named_scope("input_gradient"):

time: 195 us -> 195 us (level)
  no operation moved by 1% of the time
where the time goes in v2:
time: 195 us; the launch traced here: 194 us
  waiting for transfers between devices  58.1 us (30%)
  Pallas kernels  43.5 us (22%)
  starting transfers between devices  38.7 us (20%)
  local copies, waits for them, and re-layouts  19 us (10%)
  between operations  14.7 us (8%)
  other arithmetic  13.5 us (7%)
  matrix products  6.98 us (4%)
    ppermute x32, waiting for transfers between devices, ppermute(): return lax.ppermute(value, axis, [(i, target(i)) for i in range(16)])  54.6 us
    ppermute x32, starting transfers between devices, ppermute(): return lax.ppermute(value, axis, [(i, target(i)) for i in range(16)])  38.7 us
    unnamed x81, local copies, waits for them, and re-layouts  18.2 us
    pallas_call x2, Pallas kernels, weight_terms(): pl.pallas_call(weight_kernel, grid_spec=pltpu.PrefetchScalarGridSpec(num_...  17.8 us
    pallas_call x5, Pallas kernels, forward(): pl.pallas_call(forward_kernel, grid_spec=pltpu.PrefetchScalarGridSpec(num...  16.5 us
    pallas_call x1, Pallas kernels, scale_sum(): pl.pallas_call(scale_kernel, grid_spec=pltpu.PrefetchScalarGridSpec(num_s...  7.34 us
    dot_general x1, matrix products, backward(): lax.dot_general(dpre, w_in, (((1,), (1,)), ((), ())), preferred_element_t...  6.98 us
  transfers between devices with their start and end apart: 33, of which 11 were waited for; matrix products, arithmetic and copies ran while one was open for 6% of the time, Pallas kernels for 20%

profile of v2, /device:TPU:4, one launch (start us, length us, event | category | flops | bytes accessed | tf_op | source)
XLA Modules:
  0.0 194.5 jit_solution(4344284294075891359)
XLA Ops:
  7.2 1.2 convert_reduce_fusion
  8.4 1.3 fusion.17
  9.7 1.2 fusion.11.refs_0_
  10.9 2.0 %collective-permute-start.1 = (bf16[32,6144]{1,0:T(8,128)(2,1)S(1)}, bf16[32,6144]{1,0:T(8,128)(2,1)}, u32[]{:S(2)}, u32[]{:S(2)}) collective-permute-start(bf16[32,6144]{1,0:T(8,128)(2,1)S(1)} %fusion.11.refs_0_), channel_id=1, source_target_pairs={{0,1},{1,2},{2,3},{3,4},{4,5},{5,6},{6,7},{7,0},{8,9},{9,10},{10,1... | collective-permute-start | bytes 1179656 | tf_op jit(solution)/shard_map/gather/ppermute | solution.py:16
  12.9 4.0 %collective-permute-start = (bf16[32,6144]{1,0:T(8,128)(2,1)S(1)}, bf16[32,6144]{1,0:T(8,128)(2,1)S(1)}, u32[]{:S(2)}, u32[]{:S(2)}) collective-permute-start(bf16[32,6144]{1,0:T(8,128)(2,1)S(1)} %fusion.11.refs_0_), channel_id=1, source_target_pairs={{0,7},{1,0},{2,1},{3,2},{4,3},{5,4},{6,5},{7,6},{8,15},{9,8},{10,9... | collective-permute-start | bytes 1179656 | tf_op jit(solution)/shard_map/gather/ppermute | solution.py:16
  17.0 1.6 collective-permute-start.4
  18.5 7.6 %collective-permute-done.1.refs_2_ = bf16[32,6144]{1,0:T(8,128)(2,1)} collective-permute-done((bf16[32,6144]{1,0:T(8,128)(2,1)S(1)}, bf16[32,6144]{1,0:T(8,128)(2,1)}, u32[]{:S(2)}, u32[]{:S(2)}) %collective-permute-start.1) | collective-permute-done | bytes 393248 | tf_op jit(solution)/shard_map/gather/ppermute | solution.py:16
  26.1 3.2 %collective-permute-start.2 = (bf16[32,6144]{1,0:T(8,128)(2,1)S(1)}, bf16[32,6144]{1,0:T(8,128)(2,1)S(1)}, u32[]{:S(2)}, u32[]{:S(2)}) collective-permute-start(bf16[32,6144]{1,0:T(8,128)(2,1)S(1)} %collective-permute-done.refs_1_), channel_id=1, source_target_pairs={{0,7},{1,0},{2,1},{3,2},{4,3},{5,4},{6,5},{7,6},{8,15},{9,8},{10,9... | collective-permute-start | bytes 1179656 | tf_op jit(solution)/shard_map/gather/ppermute | solution.py:16
  29.4 1.6 collective-permute-start.9
  31.0 3.7 %copy-done = bf16[6144,768]{1,0:T(8,128)(2,1)S(1)} copy-done((bf16[6144,768]{1,0:T(8,128)(2,1)S(1)}, bf16[6144,768]{1,0:T(8,128)(2,1)}, u32[]{:S(2)}) %copy-start) | copy-done | bytes 9437208
  34.7 4.3 %forward.5.refs_16_.refs_0_ = bf16[128,768]{1,0:T(8,128)(2,1)S(1)} custom-call(s32[4]{0:T(128)S(1)} %pad_add_fusion.slots, bf16[32,6144]{1,0:T(8,128)(2,1)S(1)} %fusion.11.refs_0_, bf16[32,6144]{1,0:T(8,128)(2,1)S(1)} %collective-permute-done.refs_1_, bf16[32,6144]{1,0:T(8,128)(2,1)} %collective-permute-done.1.refs_2_, ...), custom_call_target="tpu_custom_call" | custom-call | flops 1 | bytes 1 | tf_op jit(solution)/shard_map/gather/forward/pallas_call | solution.py:120
  39.0 0.7 copy-done.20
  39.7 1.8 collective-permute-start.5
  41.5 0.3 collective-permute-start.8
  41.8 0.4 collective-permute-start.6
  42.2 0.7 pad_add_fusion.2.place
  43.1 3.7 %copy-done.1 = bf16[6144,768]{1,0:T(8,128)(2,1)S(1)} copy-done((bf16[6144,768]{1,0:T(8,128)(2,1)S(1)}, bf16[6144,768]{1,0:T(8,128)(2,1)}, u32[]{:S(2)}) %copy-start.1) | copy-done | bytes 9437208
  46.8 3.1 %forward.6.refs_17_.refs_1_ = bf16[96,768]{1,0:T(8,128)(2,1)S(1)} custom-call(s32[3]{0:T(128)S(1)} %pad_add_fusion.3.slots, bf16[32,6144]{1,0:T(8,128)(2,1)S(1)} %collective-permute-done.2.refs_0_.refs_4_, bf16[32,6144]{1,0:T(8,128)(2,1)S(1)} %collective-permute-done.3.refs_1_.refs_5_, bf16[32,6144]{1,0:T(8,128)(2,1)S(1)} %collective-permute-done.9.refs_2_.refs_6_, ...), custom_call_target="tpu_custom_call" | custom-call | flops 1 | bytes 1 | tf_op jit(solution)/shard_map/gather/forward/pallas_call | solution.py:120
  49.9 0.7 copy-done.22
  50.5 1.0 collective-permute-done.8.refs_1_.refs_8_
  51.6 2.2 %collective-permute-start.7 = (bf16[32,6144]{1,0:T(8,128)(2,1)S(1)}, bf16[32,6144]{1,0:T(8,128)(2,1)S(1)}, u32[]{:S(2)}, u32[]{:S(2)}) collective-permute-start(bf16[32,6144]{1,0:T(8,128)(2,1)S(1)} %collective-permute-done.6.refs_2_.refs_9_), channel_id=1, source_target_pairs={{0,7},{1,0},{2,1},{3,2},{4,3},{5,4},{6,5},{7,6},{8,15},{9,8},{10,9... | collective-permute-start | bytes 1179656 | tf_op jit(solution)/shard_map/gather/ppermute | solution.py:16
  53.8 1.4 collective-permute-start.11
  55.2 3.7 %copy-done.2 = bf16[6144,768]{1,0:T(8,128)(2,1)S(1)} copy-done((bf16[6144,768]{1,0:T(8,128)(2,1)S(1)}, bf16[6144,768]{1,0:T(8,128)(2,1)}, u32[]{:S(2)}) %copy-start.2) | copy-done | bytes 9437208
  58.9 3.1 %forward.7.refs_18_.refs_2_ = bf16[96,768]{1,0:T(8,128)(2,1)S(1)} custom-call(s32[3]{0:T(128)S(1)} %pad_add_fusion.4.slots, bf16[32,6144]{1,0:T(8,128)(2,1)S(1)} %collective-permute-done.5.refs_0_.refs_7_, bf16[32,6144]{1,0:T(8,128)(2,1)S(1)} %collective-permute-done.8.refs_1_.refs_8_, bf16[32,6144]{1,0:T(8,128)(2,1)S(1)} %collective-permute-done.6.refs_2_.refs_9_, ...), custom_call_target="tpu_custom_call" | custom-call | flops 1 | bytes 1 | tf_op jit(solution)/shard_map/gather/forward/pallas_call | solution.py:120
  62.0 0.7 copy-done.24
  62.7 0.3 collective-permute-done.10.refs_1_.refs_11_
  63.1 3.2 %collective-permute-start.12 = (bf16[32,6144]{1,0:T(8,128)(2,1)S(1)}, bf16[32,6144]{1,0:T(8,128)(2,1)S(1)}, u32[]{:S(2)}, u32[]{:S(2)}) collective-permute-start(bf16[32,6144]{1,0:T(8,128)(2,1)S(1)} %collective-permute-done.7.refs_0_.refs_10_), channel_id=1, source_target_pairs={{0,7},{1,0},{2,1},{3,2},{4,3},{5,4},{6,5},{7,6},{8,15},{9,8},{10,9... | collective-permute-start | bytes 1179656 | tf_op jit(solution)/shard_map/gather/ppermute | solution.py:16
  66.3 1.4 collective-permute-start.14
  68.0 3.7 %copy-done.3 = bf16[6144,768]{1,0:T(8,128)(2,1)S(1)} copy-done((bf16[6144,768]{1,0:T(8,128)(2,1)S(1)}, bf16[6144,768]{1,0:T(8,128)(2,1)}, u32[]{:S(2)}) %copy-start.3) | copy-done | bytes 9437208
  71.6 3.1 %forward.8.refs_19_.refs_3_ = bf16[96,768]{1,0:T(8,128)(2,1)S(1)} custom-call(s32[3]{0:T(128)S(1)} %pad_add_fusion.5.slots, bf16[32,6144]{1,0:T(8,128)(2,1)S(1)} %collective-permute-done.7.refs_0_.refs_10_, bf16[32,6144]{1,0:T(8,128)(2,1)S(1)} %collective-permute-done.10.refs_1_.refs_11_, bf16[32,6144]{1,0:T(8,128)(2,1)S(1)} %collective-permute-done.11.refs_2_.refs_12_, ...), custom_call_target="tpu_custom_call" | custom-call | flops 1 | bytes 1 | tf_op jit(solution)/shard_map/gather/forward/pallas_call | solution.py:120
  74.9 3.1 %forward.9.refs_20_.refs_4_ = bf16[96,768]{1,0:T(8,128)(2,1)S(1)} custom-call(s32[3]{0:T(128)S(1)} %pad_add_fusion.6.slots, bf16[32,6144]{1,0:T(8,128)(2,1)S(1)} %collective-permute-done.12.refs_0_.refs_13_, bf16[32,6144]{1,0:T(8,128)(2,1)S(1)} %collective-permute-done.13.refs_1_.refs_14_, bf16[32,6144]{1,0:T(8,128)(2,1)S(1)} %collective-permute-done.14.refs_2_.refs_15_, ...), custom_call_target="tpu_custom_call" | custom-call | flops 1 | bytes 1 | tf_op jit(solution)/shard_map/turn/forward/pallas_call | solution.py:120
  78.0 1.8 place_rows.1
  79.9 7.0 %convolution_convert_fusion.refs_16_ = bf16[512,6144]{1,0:T(8,128)(2,1)} fusion(bf16[512,768]{1,0:T(8,128)(2,1)S(1)} %place_rows.1, bf16[6144,768]{1,0:T(8,128)(2,1)S(1)} %bitcast.65), kind=kOutput, calls=%fused_computation | convolution fusion | flops 4834983936 | bytes 16515072 | tf_op jit(solution)/shard_map/turn/dot_general | solution.py:139
  86.9 0.6 slice.87.order
  87.5 7.3 %scale_sum.1 = f32[8,6144]{1,0:T(8,128)} custom-call(s32[16]{0:T(128)} %copy-done.28, bf16[32,6144]{1,0:T(8,128)(2,1)} %copy-done.5, bf16[32,6144]{1,0:T(8,128)(2,1)} %copy-done.18, bf16[32,6144]{1,0:T(8,128)(2,1)} %collective-permute-done.1.refs_2_, bf16[32,6144]{1,0:T(8,128)(2,1)} %copy-done.19, bf16[32,6144]{1,0:T(8,128)(2,1)} %copy-done.7, ...), custom_call_target="tpu_custom_call" | custom-call | flops 1 | bytes 1 | tf_op jit(solution)/shard_map/weights/scale_sum/pallas_call | solution.py:242
  94.8 1.0 reduce_sum.47
  95.8 6.7 %weight_terms.2 = (bf16[2,768,384]{2,1,0:T(8,128)(2,1)}, bf16[2,768,384]{2,1,0:T(8,128)(2,1)}) custom-call(s32[1]{0:T(128)} %bitcast.68, s32[2]{0:T(128)} %pad_add_fusion.2.place, bf16[32,6144]{1,0:T(8,128)(2,1)} %copy-done.5, bf16[32,6144]{1,0:T(8,128)(2,1)} %copy-done.18, bf16[32,6144]{1,0:T(8,128)(2,1)} %collective-permute-done.1.refs_2_, ...), custom_call_target="tpu_custom_call" | custom-call | flops 4831838208 | bytes 3932160 | tf_op jit(solution)/shard_map/weights/weight_terms/pallas_call | solution.py:175
  102.6 1.2 collective-permute-done.15
  103.8 1.3 collective-permute-start.16
  105.1 11.1 %weight_terms.3 = (bf16[6,768,384]{2,1,0:T(8,128)(2,1)}, bf16[6,768,384]{2,1,0:T(8,128)(2,1)}) custom-call(s32[3]{0:T(128)} %slice.87.order, s32[2]{0:T(128)} %pad_add_fusion.2.place, bf16[32,6144]{1,0:T(8,128)(2,1)} %copy-done.5, bf16[32,6144]{1,0:T(8,128)(2,1)} %copy-done.18, bf16[32,6144]{1,0:T(8,128)(2,1)} %collective-permute-done.1.refs_2_, ...), custom_call_target="tpu_custom_call" | custom-call | flops 14495514624 | bytes 11796480 | tf_op jit(solution)/shard_map/weights/weight_terms/pallas_call | solution.py:175
  116.3 2.8 %collective-permute-done.17 = bf16[2,768,384]{2,1,0:T(8,128)(2,1)S(1)} collective-permute-done((bf16[2,768,384]{2,1,0:T(8,128)(2,1)S(1)}, bf16[2,768,384]{2,1,0:T(8,128)(2,1)S(1)}, u32[]{:S(2)}, u32[]{:S(2)}) %collective-permute-start.17) | collective-permute-done | bytes 1179680 | tf_op jit(solution)/shard_map/core_far/ppermute | solution.py:16
  119.2 0.3 add_convert_fusion
  119.5 0.2 collective-permute-start.20
  119.9 2.0 %collective-permute-start.18 = (bf16[2,384,384]{2,1,0:T(8,128)(2,1)S(1)}, bf16[2,384,384]{2,1,0:T(8,128)(2,1)S(1)}, u32[]{:S(2)}, u32[]{:S(2)}) collective-permute-start(bf16[2,384,384]{2,1,0:T(8,128)(2,1)S(1)} %get-tuple-element.128), channel_id=1, source_target_pairs={{0,64},{16,80},{32,96},{48,112},{64,128},{80,144},{96,160},{112,17... | collective-permute-start | bytes 1769480 | tf_op jit(solution)/shard_map/x_far/ppermute | solution.py:16
  122.0 2.9 %collective-permute-start.21 = (f32[48,128]{1,0:T(8,128)S(1)}, f32[48,128]{1,0:T(8,128)S(1)}, u32[]{:S(2)}, u32[]{:S(2)}) collective-permute-start(f32[48,128]{1,0:T(8,128)S(1)} %add.350), channel_id=1, source_target_pairs={{0,32},{16,48},{32,0},{48,16},{64,96},{80,112},{96,64},{112,80},{1... | collective-permute-start | bytes 73736 | tf_op jit(solution)/shard_map/x_far/ppermute | solution.py:16
  124.9 17.9 %collective-permute-done.21 = f32[48,128]{1,0:T(8,128)S(1)} collective-permute-done((f32[48,128]{1,0:T(8,128)S(1)}, f32[48,128]{1,0:T(8,128)S(1)}, u32[]{:S(2)}, u32[]{:S(2)}) %collective-permute-start.21) | collective-permute-done | bytes 24608 | tf_op jit(solution)/shard_map/x_far/ppermute | solution.py:16
  142.9 0.7 fusion.26
  143.6 0.1 pad_maximum_fusion
  143.8 2.0 %collective-permute-start.23 = (bf16[768,384]{1,0:T(8,128)(2,1)S(1)}, bf16[768,384]{1,0:T(8,128)(2,1)S(1)}, u32[]{:S(2)}, u32[]{:S(2)}) collective-permute-start(bf16[768,384]{1,0:T(8,128)(2,1)S(1)} %get-tuple-element.100), channel_id=1, source_target_pairs={{0,192},{16,208},{32,224},{48,240},{64,0},{80,16},{96,32},{112,48}... | collective-permute-start | bytes 1769480 | tf_op jit(solution)/shard_map/x_other/ppermute | solution.py:16
  145.9 4.1 %collective-permute-done.24 = f32[48,128]{1,0:T(8,128)S(1)} collective-permute-done((f32[48,128]{1,0:T(8,128)S(1)}, f32[48,128]{1,0:T(8,128)S(1)}, u32[]{:S(2)}, u32[]{:S(2)}) %collective-permute-start.24) | collective-permute-done | bytes 24608 | tf_op jit(solution)/shard_map/x_other/ppermute | solution.py:16
  150.0 5.8 %collective-permute-done.25 = f32[48,128]{1,0:T(8,128)S(1)} collective-permute-done((f32[48,128]{1,0:T(8,128)S(1)}, f32[48,128]{1,0:T(8,128)S(1)}, u32[]{:S(2)}, u32[]{:S(2)}) %collective-permute-start.25) | collective-permute-done | bytes 24608 | tf_op jit(solution)/shard_map/x_other/ppermute | solution.py:16
  155.8 0.1 pad_maximum_fusion.2
  155.9 8.3 %collective-permute-done.26 = f32[48,128]{1,0:T(8,128)S(1)} collective-permute-done((f32[48,128]{1,0:T(8,128)S(1)}, f32[48,128]{1,0:T(8,128)S(1)}, u32[]{:S(2)}, u32[]{:S(2)}) %collective-permute-start.26) | collective-permute-done | bytes 24608 | tf_op jit(solution)/shard_map/x_other/ppermute | solution.py:16
  164.3 0.3 fusion.5
  164.7 2.3 %collective-permute-start.28 = (bf16[768,384]{1,0:T(8,128)(2,1)S(1)}, bf16[768,384]{1,0:T(8,128)(2,1)S(1)}, u32[]{:S(2)}, u32[]{:S(2)}) collective-permute-start(bf16[768,384]{1,0:T(8,128)(2,1)S(1)} %get-tuple-element.109), channel_id=1, source_target_pairs={{0,64},{16,80},{32,96},{48,112},{64,128},{80,144},{96,160},{112,17... | collective-permute-start | bytes 1769480 | tf_op jit(solution)/shard_map/x_own/ppermute | solution.py:16
  167.0 3.4 %collective-permute-start.30 = (bf16[768,384]{1,0:T(8,128)(2,1)S(1)}, bf16[768,384]{1,0:T(8,128)(2,1)}, u32[]{:S(2)}, u32[]{:S(2)}) collective-permute-start(bf16[768,384]{1,0:T(8,128)(2,1)S(1)} %fusion.5), channel_id=1, source_target_pairs={{0,32},{16,48},{32,0},{48,16},{64,96},{80,112},{96,64},{112,80},{1... | collective-permute-start | bytes 1769480 | tf_op jit(solution)/shard_map/x_own/ppermute | solution.py:16
  170.4 3.4 %reduce-scatter.2.cloned.1.call-done = bf16[32,6144]{1,0:T(8,128)(2,1)} async-done(((bf16[512,6144]{1,0:T(8,128)(2,1)}), bf16[32,6144]{1,0:T(8,128)(2,1)}) %reduce-scatter.2.cloned.1.call-update) | async-done | bytes 393232 | tf_op jit(solution)/shard_map/scatter/reduce_scatter | solution.py:314
  173.8 1.3 fusion.18
  175.1 2.1 %fusion.16 = bf16[32,6144]{1,0:T(8,128)(2,1)} fusion(bf16[32,6144]{1,0:T(8,128)(2,1)S(1)} %copy-done.29, bf16[32,6144]{1,0:T(8,128)(2,1)} %reduce-scatter.2.cloned.1.call-done, bf16[32,6144]{1,0:T(8,128)(2,1)S(1)} %copy-done.34, f32[32]{0:T(128)S(1)} %get-tuple-element.133, f32[32]{0:T(128)S(1)} %get-tuple-element.134, f32[6144]{0:T(1024)S(1)} %copy-done.33, ...), kind=kLoop, calls=%fused_computation.22 | loop fusion | flops 2359296 | bytes 1597952 | tf_op jit(solution)/shard_map/input_gradient/convert_element_type | solution.py:376
  177.2 0.8 collective-permute-start.31
  178.1 5.6 %collective-permute-done.30 = bf16[768,384]{1,0:T(8,128)(2,1)} collective-permute-done((bf16[768,384]{1,0:T(8,128)(2,1)S(1)}, bf16[768,384]{1,0:T(8,128)(2,1)}, u32[]{:S(2)}, u32[]{:S(2)}) %collective-permute-start.30) | collective-permute-done | bytes 589856 | tf_op jit(solution)/shard_map/x_own/ppermute | solution.py:16
  183.6 2.0 %fusion.3 = f32[384,768]{0,1:T(8,128)S(1)} fusion(bf16[768,384]{1,0:T(8,128)(2,1)} %collective-permute-done.30, bf16[768,384]{1,0:T(8,128)(2,1)} %collective-permute-done.29, bf16[768,384]{1,0:T(8,128)(2,1)S(1)} %collective-permute-done.28, bf16[6,768,384]{2,1,0:T(8,128)(2,1)} %copy-done.31, bf16[6,768,384]{2,1,0:T(8,128)(2,1)} %get-tuple-element.87), kind=kLoop, calls=%fused_computation.6 | loop fusion | flops 2949120 | bytes 4128768 | tf_op jit(solution)/shard_map/x_own/transpose | solution.py:364
  185.6 1.4 copy.8
  187.0 0.6 fusion.27
  (129 shorter events, 1.6 us)
Async XLA Ops:
  7.2 23.9 %copy-start.4 = (bf16[512,768]{1,0:T(8,128)(2,1)S(1)}, bf16[512,768]{1,0:T(8,128)(2,1)}, u32[]{:S(2)}) copy-start(bf16[512,768]{1,0:T(8,128)(2,1)} %refs_6_.9) | copy-start | bytes 2359300
  7.2 166.6 %reduce-scatter.2.cloned.1.call-start = ((), (), s32[]{:S(2)}) async-start(), calls=%async_computation.1 | async-start | bytes 6684672 | tf_op jit(solution)/shard_map/scatter/reduce_scatter | solution.py:314
  10.9 28.0 %copy-start.5 = (bf16[32,6144]{1,0:T(8,128)(2,1)}, bf16[32,6144]{1,0:T(8,128)(2,1)S(1)}, u32[]{:S(2)}) copy-start(bf16[32,6144]{1,0:T(8,128)(2,1)S(1)} %fusion.11.refs_0_) | copy-start | bytes 1179652
  10.9 15.2 %collective-permute-start.1 = (bf16[32,6144]{1,0:T(8,128)(2,1)S(1)}, bf16[32,6144]{1,0:T(8,128)(2,1)}, u32[]{:S(2)}, u32[]{:S(2)}) collective-permute-start(bf16[32,6144]{1,0:T(8,128)(2,1)S(1)} %fusion.11.refs_0_), channel_id=1, source_target_pairs={{0,1},{1,2},{2,3},{3,4},{4,5},{5,6},{6,7},{7,0},{8,9},{9,10},{10,1... | collective-permute-start | bytes 1179656 | tf_op jit(solution)/shard_map/gather/ppermute | solution.py:16
  12.9 13.2 %collective-permute-start = (bf16[32,6144]{1,0:T(8,128)(2,1)S(1)}, bf16[32,6144]{1,0:T(8,128)(2,1)S(1)}, u32[]{:S(2)}, u32[]{:S(2)}) collective-permute-start(bf16[32,6144]{1,0:T(8,128)(2,1)S(1)} %fusion.11.refs_0_), channel_id=1, source_target_pairs={{0,7},{1,0},{2,1},{3,2},{4,3},{5,4},{6,5},{7,6},{8,15},{9,8},{10,9... | collective-permute-start | bytes 1179656 | tf_op jit(solution)/shard_map/gather/ppermute | solution.py:16
  17.0 14.1 %collective-permute-start.4 = (bf16[32,6144]{1,0:T(8,128)(2,1)S(1)}, bf16[32,6144]{1,0:T(8,128)(2,1)S(1)}, u32[]{:S(2)}, u32[]{:S(2)}) collective-permute-start(bf16[32,6144]{1,0:T(8,128)(2,1)S(1)} %fusion.11.refs_0_), channel_id=1, source_target_pairs={{0,8},{1,9},{2,10},{3,11},{4,12},{5,13},{6,14},{7,15},{8,0},{9,1},... | collective-permute-start | bytes 1179656 | tf_op jit(solution)/shard_map/gather/ppermute | solution.py:16
  26.1 12.9 %copy-start.18 = (bf16[32,6144]{1,0:T(8,128)(2,1)}, bf16[32,6144]{1,0:T(8,128)(2,1)S(1)}, u32[]{:S(2)}) copy-start(bf16[32,6144]{1,0:T(8,128)(2,1)S(1)} %collective-permute-done.refs_1_) | copy-start | bytes 1179652
  26.1 13.6 %collective-permute-start.3 = (bf16[32,6144]{1,0:T(8,128)(2,1)}, bf16[32,6144]{1,0:T(8,128)(2,1)S(1)}, u32[]{:S(2)}, u32[]{:S(2)}) collective-permute-start(bf16[32,6144]{1,0:T(8,128)(2,1)} %collective-permute-done.1.refs_2_), channel_id=1, source_target_pairs={{0,1},{1,2},{2,3},{3,4},{4,5},{5,6},{6,7},{7,0},{8,9},{9,10},{10,1... | collective-permute-start | bytes 1179656 | tf_op jit(solution)/shard_map/gather/ppermute | solution.py:16
  26.1 13.6 %collective-permute-start.2 = (bf16[32,6144]{1,0:T(8,128)(2,1)S(1)}, bf16[32,6144]{1,0:T(8,128)(2,1)S(1)}, u32[]{:S(2)}, u32[]{:S(2)}) collective-permute-start(bf16[32,6144]{1,0:T(8,128)(2,1)S(1)} %collective-permute-done.refs_1_), channel_id=1, source_target_pairs={{0,7},{1,0},{2,1},{3,2},{4,3},{5,4},{6,5},{7,6},{8,15},{9,8},{10,9... | collective-permute-start | bytes 1179656 | tf_op jit(solution)/shard_map/gather/ppermute | solution.py:16
  29.4 13.7 %collective-permute-start.9 = (bf16[32,6144]{1,0:T(8,128)(2,1)S(1)}, bf16[32,6144]{1,0:T(8,128)(2,1)S(1)}, u32[]{:S(2)}, u32[]{:S(2)}) collective-permute-start(bf16[32,6144]{1,0:T(8,128)(2,1)S(1)} %collective-permute-done.refs_1_), channel_id=1, source_target_pairs={{0,8},{1,9},{2,10},{3,11},{4,12},{5,13},{6,14},{7,15},{8,0},{9,1},... | collective-permute-start | bytes 1179656 | tf_op jit(solution)/shard_map/gather/ppermute | solution.py:16
  31.0 3.7 %copy-start = (bf16[6144,768]{1,0:T(8,128)(2,1)S(1)}, bf16[6144,768]{1,0:T(8,128)(2,1)}, u32[]{:S(2)}) copy-start(bf16[6144,768]{1,0:T(8,128)(2,1)} %refs_3_.7) | copy-start | bytes 28311556
  34.7 4.3 %copy-start.19 = (bf16[32,6144]{1,0:T(8,128)(2,1)}, bf16[32,6144]{1,0:T(8,128)(2,1)S(1)}, u32[]{:S(2)}) copy-start(bf16[32,6144]{1,0:T(8,128)(2,1)S(1)} %collective-permute-done.4.refs_3_) | copy-start | bytes 1179652
  39.7 14.1 %copy-start.6 = (bf16[32,6144]{1,0:T(8,128)(2,1)}, bf16[32,6144]{1,0:T(8,128)(2,1)S(1)}, u32[]{:S(2)}) copy-start(bf16[32,6144]{1,0:T(8,128)(2,1)S(1)} %collective-permute-done.3.refs_1_.refs_5_) | copy-start | bytes 1179652
  39.7 10.1 %copy-start.7 = (bf16[32,6144]{1,0:T(8,128)(2,1)}, bf16[32,6144]{1,0:T(8,128)(2,1)S(1)}, u32[]{:S(2)}) copy-start(bf16[32,6144]{1,0:T(8,128)(2,1)S(1)} %collective-permute-done.2.refs_0_.refs_4_) | copy-start | bytes 1179652
  39.7 10.8 %collective-permute-start.5 = (bf16[32,6144]{1,0:T(8,128)(2,1)S(1)}, bf16[32,6144]{1,0:T(8,128)(2,1)S(1)}, u32[]{:S(2)}, u32[]{:S(2)}) collective-permute-start(bf16[32,6144]{1,0:T(8,128)(2,1)S(1)} %collective-permute-done.2.refs_0_.refs_4_), channel_id=1, source_target_pairs={{0,7},{1,0},{2,1},{3,2},{4,3},{5,4},{6,5},{7,6},{8,15},{9,8},{10,9... | collective-permute-start | bytes 1179656 | tf_op jit(solution)/shard_map/gather/ppermute | solution.py:16
  41.5 10.1 %collective-permute-start.8 = (bf16[32,6144]{1,0:T(8,128)(2,1)S(1)}, bf16[32,6144]{1,0:T(8,128)(2,1)S(1)}, u32[]{:S(2)}, u32[]{:S(2)}) collective-permute-start(bf16[32,6144]{1,0:T(8,128)(2,1)S(1)} %collective-permute-done.3.refs_1_.refs_5_), channel_id=1, source_target_pairs={{0,1},{1,2},{2,3},{3,4},{4,5},{5,6},{6,7},{7,0},{8,9},{9,10},{10,1... | collective-permute-start | bytes 1179656 | tf_op jit(solution)/shard_map/gather/ppermute | solution.py:16
  41.8 9.8 %collective-permute-start.6 = (bf16[32,6144]{1,0:T(8,128)(2,1)S(1)}, bf16[32,6144]{1,0:T(8,128)(2,1)S(1)}, u32[]{:S(2)}, u32[]{:S(2)}) collective-permute-start(bf16[32,6144]{1,0:T(8,128)(2,1)S(1)} %collective-permute-done.2.refs_0_.refs_4_), channel_id=1, source_target_pairs={{0,8},{1,9},{2,10},{3,11},{4,12},{5,13},{6,14},{7,15},{8,0},{9,1},... | collective-permute-start | bytes 1179656 | tf_op jit(solution)/shard_map/gather/ppermute | solution.py:16
  43.1 43.8 %copy-start.35 = (s32[4]{0:T(128)}, s32[4]{0:T(128)S(1)}, u32[]{:S(2)}) copy-start(s32[4]{0:T(128)S(1)} %pad_add_fusion.1) | copy-start | bytes 52
  43.1 3.7 %copy-start.1 = (bf16[6144,768]{1,0:T(8,128)(2,1)S(1)}, bf16[6144,768]{1,0:T(8,128)(2,1)}, u32[]{:S(2)}) copy-start(bf16[6144,768]{1,0:T(8,128)(2,1)} %refs_3_.7) | copy-start | bytes 28311556
  50.5 11.5 %copy-start.9 = (bf16[32,6144]{1,0:T(8,128)(2,1)}, bf16[32,6144]{1,0:T(8,128)(2,1)S(1)}, u32[]{:S(2)}) copy-start(bf16[32,6144]{1,0:T(8,128)(2,1)S(1)} %collective-permute-done.5.refs_0_.refs_7_) | copy-start | bytes 1179652
  51.6 10.4 %copy-start.10 = (bf16[32,6144]{1,0:T(8,128)(2,1)}, bf16[32,6144]{1,0:T(8,128)(2,1)S(1)}, u32[]{:S(2)}) copy-start(bf16[32,6144]{1,0:T(8,128)(2,1)S(1)} %collective-permute-done.8.refs_1_.refs_8_) | copy-start | bytes 1179652
  51.6 10.4 %copy-start.11 = (bf16[32,6144]{1,0:T(8,128)(2,1)}, bf16[32,6144]{1,0:T(8,128)(2,1)S(1)}, u32[]{:S(2)}) copy-start(bf16[32,6144]{1,0:T(8,128)(2,1)S(1)} %collective-permute-done.6.refs_2_.refs_9_) | copy-start | bytes 1179652
  51.6 11.1 %collective-permute-start.7 = (bf16[32,6144]{1,0:T(8,128)(2,1)S(1)}, bf16[32,6144]{1,0:T(8,128)(2,1)S(1)}, u32[]{:S(2)}, u32[]{:S(2)}) collective-permute-start(bf16[32,6144]{1,0:T(8,128)(2,1)S(1)} %collective-permute-done.6.refs_2_.refs_9_), channel_id=1, source_target_pairs={{0,7},{1,0},{2,1},{3,2},{4,3},{5,4},{6,5},{7,6},{8,15},{9,8},{10,9... | collective-permute-start | bytes 1179656 | tf_op jit(solution)/shard_map/gather/ppermute | solution.py:16
  53.8 9.2 %collective-permute-start.10 = (bf16[32,6144]{1,0:T(8,128)(2,1)S(1)}, bf16[32,6144]{1,0:T(8,128)(2,1)S(1)}, u32[]{:S(2)}, u32[]{:S(2)}) collective-permute-start(bf16[32,6144]{1,0:T(8,128)(2,1)S(1)} %collective-permute-done.8.refs_1_.refs_8_), channel_id=1, source_target_pairs={{0,1},{1,2},{2,3},{3,4},{4,5},{5,6},{6,7},{7,0},{8,9},{9,10},{10,1... | collective-permute-start | bytes 1179656 | tf_op jit(solution)/shard_map/gather/ppermute | solution.py:16
  53.8 9.2 %collective-permute-start.11 = (bf16[32,6144]{1,0:T(8,128)(2,1)S(1)}, bf16[32,6144]{1,0:T(8,128)(2,1)S(1)}, u32[]{:S(2)}, u32[]{:S(2)}) collective-permute-start(bf16[32,6144]{1,0:T(8,128)(2,1)S(1)} %collective-permute-done.3.refs_1_.refs_5_), channel_id=1, source_target_pairs={{0,8},{1,9},{2,10},{3,11},{4,12},{5,13},{6,14},{7,15},{8,0},{9,1},... | collective-permute-start | bytes 1179656 | tf_op jit(solution)/shard_map/gather/ppermute | solution.py:16
  55.2 3.7 %copy-start.2 = (bf16[6144,768]{1,0:T(8,128)(2,1)S(1)}, bf16[6144,768]{1,0:T(8,128)(2,1)}, u32[]{:S(2)}) copy-start(bf16[6144,768]{1,0:T(8,128)(2,1)} %refs_3_.7) | copy-start | bytes 28311556
  62.7 12.0 %copy-start.12 = (bf16[32,6144]{1,0:T(8,128)(2,1)}, bf16[32,6144]{1,0:T(8,128)(2,1)S(1)}, u32[]{:S(2)}) copy-start(bf16[32,6144]{1,0:T(8,128)(2,1)S(1)} %collective-permute-done.7.refs_0_.refs_10_) | copy-start | bytes 1179652
  63.0 11.8 %copy-start.13 = (bf16[32,6144]{1,0:T(8,128)(2,1)}, bf16[32,6144]{1,0:T(8,128)(2,1)S(1)}, u32[]{:S(2)}) copy-start(bf16[32,6144]{1,0:T(8,128)(2,1)S(1)} %collective-permute-done.10.refs_1_.refs_11_) | copy-start | bytes 1179652
  63.0 11.8 %copy-start.14 = (bf16[32,6144]{1,0:T(8,128)(2,1)}, bf16[32,6144]{1,0:T(8,128)(2,1)S(1)}, u32[]{:S(2)}) copy-start(bf16[32,6144]{1,0:T(8,128)(2,1)S(1)} %collective-permute-done.11.refs_2_.refs_12_) | copy-start | bytes 1179652
  63.0 11.8 %collective-permute-start.13 = (bf16[32,6144]{1,0:T(8,128)(2,1)S(1)}, bf16[32,6144]{1,0:T(8,128)(2,1)S(1)}, u32[]{:S(2)}, u32[]{:S(2)}) collective-permute-start(bf16[32,6144]{1,0:T(8,128)(2,1)S(1)} %collective-permute-done.11.refs_2_.refs_12_), channel_id=1, source_target_pairs={{0,1},{1,2},{2,3},{3,4},{4,5},{5,6},{6,7},{7,0},{8,9},{9,10},{10,1... | collective-permute-start | bytes 1179656 | tf_op jit(solution)/shard_map/gather/ppermute | solution.py:16
  63.1 11.8 %collective-permute-start.12 = (bf16[32,6144]{1,0:T(8,128)(2,1)S(1)}, bf16[32,6144]{1,0:T(8,128)(2,1)S(1)}, u32[]{:S(2)}, u32[]{:S(2)}) collective-permute-start(bf16[32,6144]{1,0:T(8,128)(2,1)S(1)} %collective-permute-done.7.refs_0_.refs_10_), channel_id=1, source_target_pairs={{0,7},{1,0},{2,1},{3,2},{4,3},{5,4},{6,5},{7,6},{8,15},{9,8},{10,9... | collective-permute-start | bytes 1179656 | tf_op jit(solution)/shard_map/gather/ppermute | solution.py:16
  66.3 8.5 %collective-permute-start.14 = (bf16[32,6144]{1,0:T(8,128)(2,1)}, bf16[32,6144]{1,0:T(8,128)(2,1)S(1)}, u32[]{:S(2)}, u32[]{:S(2)}) collective-permute-start(bf16[32,6144]{1,0:T(8,128)(2,1)} %collective-permute-done.1.refs_2_), channel_id=1, source_target_pairs={{0,8},{1,9},{2,10},{3,11},{4,12},{5,13},{6,14},{7,15},{8,0},{9,1},... | collective-permute-start | bytes 1179656 | tf_op jit(solution)/shard_map/gather/ppermute | solution.py:16
  67.8 10.2 %copy-start.28 = (s32[16]{0:T(128)}, s32[16]{0:T(128)S(1)}, u32[]{:S(2)}) copy-start(s32[16]{0:T(128)S(1)} %stack.135.slots) | copy-start | bytes 196
  68.0 3.7 %copy-start.3 = (bf16[6144,768]{1,0:T(8,128)(2,1)S(1)}, bf16[6144,768]{1,0:T(8,128)(2,1)}, u32[]{:S(2)}) copy-start(bf16[6144,768]{1,0:T(8,128)(2,1)} %refs_3_.7) | copy-start | bytes 28311556
  71.6 8.2 %slice-start = ((s8[9437184]{0:T(1024)(128)(4,1)}), s8[4194304]{0:T(1024)(128)(4,1)S(1)}, s32[]{:S(2)}) async-start(s8[9437184]{0:T(1024)(128)(4,1)} %bitcast.64), calls=%async_computation.2 | async-start | bytes 8388608
  71.6 8.2 %slice-start.1 = ((s8[9437184]{0:T(1024)(128)(4,1)}), s8[4194304]{0:T(1024)(128)(4,1)S(1)}, s32[]{:S(2)}) async-start(s8[9437184]{0:T(1024)(128)(4,1)} %bitcast.64), calls=%async_computation.3 | async-start | bytes 8388608
  74.8 3.2 %copy-start.21 = (bf16[128,768]{1,0:T(8,128)(2,1)S(1)}, bf16[128,768]{1,0:T(8,128)(2,1)}, u32[]{:S(2)}) copy-start(bf16[128,768]{1,0:T(8,128)(2,1)} %copy-done.20) | copy-start | bytes 589828
  74.8 3.2 %copy-start.23 = (bf16[96,768]{1,0:T(8,128)(2,1)S(1)}, bf16[96,768]{1,0:T(8,128)(2,1)}, u32[]{:S(2)}) copy-start(bf16[96,768]{1,0:T(8,128)(2,1)} %copy-done.22) | copy-start | bytes 442372
  74.8 5.1 %slice-start.2 = ((s8[9437184]{0:T(1024)(128)(4,1)}), s8[1048576]{0:T(1024)(128)(4,1)S(1)}, s32[]{:S(2)}) async-start(s8[9437184]{0:T(1024)(128)(4,1)} %bitcast.64), calls=%async_computation.4 | async-start | bytes 2097152
  78.0 8.8 %copy-start.27 = (bf16[96,768]{1,0:T(8,128)(2,1)}, bf16[96,768]{1,0:T(8,128)(2,1)S(1)}, u32[]{:S(2)}) copy-start(bf16[96,768]{1,0:T(8,128)(2,1)S(1)} %forward.9.refs_20_.refs_4_) | copy-start | bytes 442372
  102.5 1.3 collective-permute-start.15
  103.8 12.4 %copy-start.36 = (bf16[2,768,384]{2,1,0:T(8,128)(2,1)S(1)}, bf16[2,768,384]{2,1,0:T(8,128)(2,1)}, u32[]{:S(2)}) copy-start(bf16[2,768,384]{2,1,0:T(8,128)(2,1)} %get-tuple-element.89) | copy-start | bytes 3538948
  103.8 15.4 %copy-start.32 = (bf16[2,768,384]{2,1,0:T(8,128)(2,1)S(1)}, bf16[2,768,384]{2,1,0:T(8,128)(2,1)}, u32[]{:S(2)}) copy-start(bf16[2,768,384]{2,1,0:T(8,128)(2,1)} %get-tuple-element.88) | copy-start | bytes 3538948
  103.8 12.4 %collective-permute-start.16 = (f32[48,128]{1,0:T(8,128)S(1)}, f32[48,128]{1,0:T(8,128)S(1)}, u32[]{:S(2)}, u32[]{:S(2)}) collective-permute-start(f32[48,128]{1,0:T(8,128)S(1)} %add.349), channel_id=1, source_target_pairs={{0,64},{16,80},{32,96},{48,112},{64,0},{80,16},{96,32},{112,48},{1... | collective-permute-start | bytes 73736 | tf_op jit(solution)/shard_map/weights/ppermute | solution.py:16
  116.2 2.9 %collective-permute-start.17 = (bf16[2,768,384]{2,1,0:T(8,128)(2,1)S(1)}, bf16[2,768,384]{2,1,0:T(8,128)(2,1)S(1)}, u32[]{:S(2)}, u32[]{:S(2)}) collective-permute-start(bf16[2,768,384]{2,1,0:T(8,128)(2,1)S(1)} %copy-done.36), channel_id=1, source_target_pairs={{0,16},{16,0},{32,48},{48,32},{64,80},{80,64},{96,112},{112,96},{1... | collective-permute-start | bytes 3538952 | tf_op jit(solution)/shard_map/core_far/ppermute | solution.py:16
  119.2 23.6 %copy-start.30 = (bf16[6,768,384]{2,1,0:T(8,128)(2,1)S(1)}, bf16[6,768,384]{2,1,0:T(8,128)(2,1)}, u32[]{:S(2)}) copy-start(bf16[6,768,384]{2,1,0:T(8,128)(2,1)} %get-tuple-element.87) | copy-start | bytes 10616836
  119.5 23.3 %collective-permute-start.20 = (bf16[6,768,384]{2,1,0:T(8,128)(2,1)}, bf16[6,768,384]{2,1,0:T(8,128)(2,1)S(1)}, u32[]{:S(2)}, u32[]{:S(2)}) collective-permute-start(bf16[6,768,384]{2,1,0:T(8,128)(2,1)} %get-tuple-element.93), channel_id=1, source_target_pairs={{0,16},{16,0},{32,48},{48,32},{64,80},{80,64},{96,112},{112,96},{1... | collective-permute-start | bytes 10616840 | tf_op jit(solution)/shard_map/x_far/ppermute | solution.py:16
  119.8 22.9 %collective-permute-start.19 = (bf16[2,384,384]{2,1,0:T(8,128)(2,1)S(1)}, bf16[2,384,384]{2,1,0:T(8,128)(2,1)S(1)}, u32[]{:S(2)}, u32[]{:S(2)}) collective-permute-start(bf16[2,384,384]{2,1,0:T(8,128)(2,1)S(1)} %get-tuple-element.127), channel_id=1, source_target_pairs={{0,192},{16,208},{32,224},{48,240},{64,0},{80,16},{96,32},{112,48}... | collective-permute-start | bytes 1769480 | tf_op jit(solution)/shard_map/x_far/ppermute | solution.py:16
  119.9 22.8 %collective-permute-start.18 = (bf16[2,384,384]{2,1,0:T(8,128)(2,1)S(1)}, bf16[2,384,384]{2,1,0:T(8,128)(2,1)S(1)}, u32[]{:S(2)}, u32[]{:S(2)}) collective-permute-start(bf16[2,384,384]{2,1,0:T(8,128)(2,1)S(1)} %get-tuple-element.128), channel_id=1, source_target_pairs={{0,64},{16,80},{32,96},{48,112},{64,128},{80,144},{96,160},{112,17... | collective-permute-start | bytes 1769480 | tf_op jit(solution)/shard_map/x_far/ppermute | solution.py:16
  122.0 20.8 %collective-permute-start.21 = (f32[48,128]{1,0:T(8,128)S(1)}, f32[48,128]{1,0:T(8,128)S(1)}, u32[]{:S(2)}, u32[]{:S(2)}) collective-permute-start(f32[48,128]{1,0:T(8,128)S(1)} %add.350), channel_id=1, source_target_pairs={{0,32},{16,48},{32,0},{48,16},{64,96},{80,112},{96,64},{112,80},{1... | collective-permute-start | bytes 73736 | tf_op jit(solution)/shard_map/x_far/ppermute | solution.py:16
  142.8 21.5 %copy-start.31 = (bf16[6,768,384]{2,1,0:T(8,128)(2,1)}, bf16[6,768,384]{2,1,0:T(8,128)(2,1)S(1)}, u32[]{:S(2)}) copy-start(bf16[6,768,384]{2,1,0:T(8,128)(2,1)S(1)} %collective-permute-done.20) | copy-start | bytes 10616836
  143.8 20.5 %collective-permute-start.22 = (bf16[768,384]{1,0:T(8,128)(2,1)S(1)}, bf16[768,384]{1,0:T(8,128)(2,1)S(1)}, u32[]{:S(2)}, u32[]{:S(2)}) collective-permute-start(bf16[768,384]{1,0:T(8,128)(2,1)S(1)} %get-tuple-element.99), channel_id=1, source_target_pairs={{0,64},{16,80},{32,96},{48,112},{64,128},{80,144},{96,160},{112,17... | collective-permute-start | bytes 1769480 | tf_op jit(solution)/shard_map/x_other/ppermute | solution.py:16
  143.8 20.4 %collective-permute-start.23 = (bf16[768,384]{1,0:T(8,128)(2,1)S(1)}, bf16[768,384]{1,0:T(8,128)(2,1)S(1)}, u32[]{:S(2)}, u32[]{:S(2)}) collective-permute-start(bf16[768,384]{1,0:T(8,128)(2,1)S(1)} %get-tuple-element.100), channel_id=1, source_target_pairs={{0,192},{16,208},{32,224},{48,240},{64,0},{80,16},{96,32},{112,48}... | collective-permute-start | bytes 1769480 | tf_op jit(solution)/shard_map/x_other/ppermute | solution.py:16
  145.9 4.2 %collective-permute-start.24 = (f32[48,128]{1,0:T(8,128)S(1)}, f32[48,128]{1,0:T(8,128)S(1)}, u32[]{:S(2)}, u32[]{:S(2)}) collective-permute-start(f32[48,128]{1,0:T(8,128)S(1)} %add.352), channel_id=1, source_target_pairs={{0,1},{1,0},{2,3},{3,2},{4,5},{5,4},{6,7},{7,6},{8,9},{9,8},{10,11... | collective-permute-start | bytes 73736 | tf_op jit(solution)/shard_map/x_other/ppermute | solution.py:16
  150.0 5.8 %collective-permute-start.25 = (f32[48,128]{1,0:T(8,128)S(1)}, f32[48,128]{1,0:T(8,128)S(1)}, u32[]{:S(2)}, u32[]{:S(2)}) collective-permute-start(f32[48,128]{1,0:T(8,128)S(1)} %add.365), channel_id=1, source_target_pairs={{0,2},{1,3},{2,0},{3,1},{4,6},{5,7},{6,4},{7,5},{8,10},{9,11},{10,... | collective-permute-start | bytes 73736 | tf_op jit(solution)/shard_map/x_other/ppermute | solution.py:16
  155.8 8.4 %collective-permute-start.26 = (f32[48,128]{1,0:T(8,128)S(1)}, f32[48,128]{1,0:T(8,128)S(1)}, u32[]{:S(2)}, u32[]{:S(2)}) collective-permute-start(f32[48,128]{1,0:T(8,128)S(1)} %add.366), channel_id=1, source_target_pairs={{0,4},{1,5},{2,6},{3,7},{4,0},{5,1},{6,2},{7,3},{8,12},{9,13},{10,... | collective-permute-start | bytes 73736 | tf_op jit(solution)/shard_map/x_other/ppermute | solution.py:16
  164.3 9.5 %copy-start.29 = (bf16[32,6144]{1,0:T(8,128)(2,1)S(1)}, bf16[32,6144]{1,0:T(8,128)(2,1)}, u32[]{:S(2)}) copy-start(bf16[32,6144]{1,0:T(8,128)(2,1)} %param.5) | copy-start | bytes 1179652
  164.3 9.5 %copy-start.33 = (f32[6144]{0:T(1024)S(1)}, f32[6144]{0:T(1024)}, u32[]{:S(2)}) copy-start(f32[6144]{0:T(1024)} %param.6) | copy-start | bytes 73732
  164.3 10.8 %copy-start.34 = (bf16[32,6144]{1,0:T(8,128)(2,1)S(1)}, bf16[32,6144]{1,0:T(8,128)(2,1)}, u32[]{:S(2)}) copy-start(bf16[32,6144]{1,0:T(8,128)(2,1)} %param.9) | copy-start | bytes 1179652
  164.6 12.6 %collective-permute-start.27 = (f32[48,128]{1,0:T(8,128)S(1)}, f32[48,128]{1,0:T(8,128)S(1)}, u32[]{:S(2)}, u32[]{:S(2)}) collective-permute-start(f32[48,128]{1,0:T(8,128)S(1)} %add.367), channel_id=1, source_target_pairs={{0,128},{16,144},{32,160},{48,176},{64,192},{80,208},{96,224},{112... | collective-permute-start | bytes 73736 | tf_op jit(solution)/shard_map/x_own/ppermute | solution.py:16
  164.7 13.4 %collective-permute-start.28 = (bf16[768,384]{1,0:T(8,128)(2,1)S(1)}, bf16[768,384]{1,0:T(8,128)(2,1)S(1)}, u32[]{:S(2)}, u32[]{:S(2)}) collective-permute-start(bf16[768,384]{1,0:T(8,128)(2,1)S(1)} %get-tuple-element.109), channel_id=1, source_target_pairs={{0,64},{16,80},{32,96},{48,112},{64,128},{80,144},{96,160},{112,17... | collective-permute-start | bytes 1769480 | tf_op jit(solution)/shard_map/x_own/ppermute | solution.py:16
  167.0 11.1 %collective-permute-start.29 = (bf16[768,384]{1,0:T(8,128)(2,1)S(1)}, bf16[768,384]{1,0:T(8,128)(2,1)}, u32[]{:S(2)}, u32[]{:S(2)}) collective-permute-start(bf16[768,384]{1,0:T(8,128)(2,1)S(1)} %get-tuple-element.110), channel_id=1, source_target_pairs={{0,192},{16,208},{32,224},{48,240},{64,0},{80,16},{96,32},{112,48}... | collective-permute-start | bytes 1769480 | tf_op jit(solution)/shard_map/x_own/ppermute | solution.py:16
  167.0 16.7 %collective-permute-start.30 = (bf16[768,384]{1,0:T(8,128)(2,1)S(1)}, bf16[768,384]{1,0:T(8,128)(2,1)}, u32[]{:S(2)}, u32[]{:S(2)}) collective-permute-start(bf16[768,384]{1,0:T(8,128)(2,1)S(1)} %fusion.5), channel_id=1, source_target_pairs={{0,32},{16,48},{32,0},{48,16},{64,96},{80,112},{96,64},{112,80},{1... | collective-permute-start | bytes 1769480 | tf_op jit(solution)/shard_map/x_own/ppermute | solution.py:16
  177.2 9.8 %collective-permute-start.31 = (f32[48,128]{1,0:T(8,128)S(1)}, f32[48,128]{1,0:T(8,128)S(1)}, u32[]{:S(2)}, u32[]{:S(2)}) collective-permute-start(f32[48,128]{1,0:T(8,128)S(1)} %add.378), channel_id=1, source_target_pairs={{0,8},{1,9},{2,10},{3,11},{4,12},{5,13},{6,14},{7,15},{8,0},{9,1},... | collective-permute-start | bytes 73736 | tf_op jit(solution)/shard_map/scale_gradient/ppermute | solution.py:16
  (9 other events, 21.0 us)
Sparse Core Ops, SparseCore 0:
  87.0 86.7 reduce-scatter.1
